TPU v7x, 128 devices: a whole 4x4x4 slice. The times are simulated.
128 devices in a mesh: group: 2 (over x_lo), shard: 64 (over z, x_hi, y, core).
Axes of the slice: x: 4 (x_hi: 2, x_lo: 2; x = x_hi * 2 + x_lo), y: 4, z: 4, core: 2. Of those that a mesh axis runs over, the one named last changes fastest.
Arguments:
- replica_weights: bfloat16 [2, 64, 512, 2048], P('group', None, 'shard'), may hold values from -6 to 6
- anchor_slabs: float32 [64, 2, 512, 2048], P('shard', None, None, 'group'), may hold values from -6 to 6
- momentum_slabs: float32 [64, 2, 512, 2048], P('shard', None, None, 'group'), may hold values from -4 to 4
- slab_owner: int32 [64], replicated, may hold values from 0 to 63, as said below
- replica_embed: bfloat16 [2, 768, 512], P('group', 'shard'), may hold values from -6 to 6
- anchor_embed: float32 [768, 512], P('shard'), may hold values from -6 to 6
- momentum_embed: float32 [768, 512], P('shard'), may hold values from -4 to 4
- embed_basis: float32 [768, 64], P('shard'), may hold values from -0.21875 to 0.21875
Outputs:
- new_anchor_slabs: float32 [64, 2, 512, 2048], P('shard', None, None, 'group')
- new_momentum_slabs: float32 [64, 2, 512, 2048], P('shard', None, None, 'group')
- new_weights: bfloat16 [2, 64, 512, 2048], P('group', None, 'shard')
- new_anchor_embed: float32 [768, 512], P('shard')
- new_momentum_embed: float32 [768, 512], P('shard')
- new_embed_weights: bfloat16 [2, 768, 512], P('group', 'shard')
Inputs may be any that keep to these rules, and one draw needn't show every extreme that they name: `slab_owner`: of the devices of shard, a quarter own 2 matrices each, half own 1 each and a quarter own none.
All inputs are finite; a program needn't handle non-finite values.
Results may differ from a plain program's by a relative error of at most 0.008.
Values may be sent and summed in bfloat16 or wider, within the bound.
A program may use at most 128 MiB of HBM per device.

v0:
```python
import jax
import jax.numpy as jnp
from jax import lax
from jax.sharding import PartitionSpec as P

OUTER_RATE = 0.7
MOMENTUM_COEF = 0.9


def slot_tables(slab_owner, devices, capacity):
    slab_count = slab_owner.shape[0]
    order_ids = jnp.arange(slab_count, dtype=jnp.int32)
    same_owner = slab_owner[:, None] == slab_owner[None, :]
    earlier = order_ids[None, :] < order_ids[:, None]
    slot_index = jnp.sum((same_owner & earlier).astype(jnp.int32), axis=1)
    matches = (slab_owner[:, None, None] == jnp.arange(devices, dtype=jnp.int32)[None, :, None]) & (
        slot_index[:, None, None] == jnp.arange(capacity, dtype=jnp.int32)[None, None, :]
    )
    slab_of = jnp.sum(jnp.where(matches, order_ids[:, None, None], 0), axis=0)
    slot_used = jnp.any(matches, axis=0)
    return (slot_index, slab_of, slot_used)


def nesterov(anchor_value, moment, mean_value):
    outer_grad = anchor_value - mean_value
    new_moment = MOMENTUM_COEF * moment + outer_grad
    new_anchor = anchor_value - OUTER_RATE * (outer_grad + MOMENTUM_COEF * new_moment)
    return (new_anchor, new_moment)


def on_device(
    replica_weights,
    anchor_slabs,
    momentum_slabs,
    slab_owner,
    replica_embed,
    anchor_embed,
    momentum_embed,
    embed_basis,
):
    local_rows = replica_weights[0]
    row_count = local_rows.shape[1]
    width = local_rows.shape[2]
    devices = lax.axis_size("shard")
    n_group = lax.axis_size("group")
    capacity = anchor_slabs.shape[1]
    slot_index, slab_of, slot_used = slot_tables(slab_owner, devices, capacity)
    send_ids = slab_of.T.reshape(-1)
    send_used = slot_used.T
    back_ids = slot_index * devices + slab_owner
    owner_here = lax.axis_index("shard")
    my_used = lax.dynamic_index_in_dim(slot_used, owner_here, 0, keepdims=False)
    anchor_here = anchor_slabs[0]
    moment_here = momentum_slabs[0]
    picked = jnp.take(local_rows, send_ids, axis=0)
    picked = picked.reshape(capacity, devices, local_rows.shape[1], local_rows.shape[2])
    received = lax.all_to_all(
        jnp.where(send_used[:, :, None, None], picked, jnp.zeros((), local_rows.dtype)),
        "shard",
        split_axis=1,
        concat_axis=1,
        tiled=True,
    )
    gathered = received.reshape(capacity, devices * received.shape[2], received.shape[3])
    summed = lax.psum_scatter(
        gathered.astype(jnp.float32).astype(jnp.bfloat16), "group", scatter_dimension=2, tiled=True
    ).astype(jnp.float32)
    new_anchor, new_moment = nesterov(anchor_here, moment_here, summed / n_group)
    keep = my_used[:, None, None]
    new_anchor = jnp.where(keep, new_anchor, anchor_here)
    new_moment = jnp.where(keep, new_moment, moment_here)
    new_half = new_anchor.astype(jnp.bfloat16)
    full_cols = lax.all_gather(new_half, "group", axis=2, tiled=True)
    split_rows = full_cols.reshape(capacity, devices, row_count, width)
    received = lax.all_to_all(split_rows, "shard", split_axis=1, concat_axis=1, tiled=True)
    flat_rows = received.reshape(capacity * devices, received.shape[2], received.shape[3])
    new_rows = jnp.take(flat_rows, back_ids, axis=0)
    embed_here = replica_embed[0].astype(jnp.float32)
    partial_factor = jnp.dot(
        embed_basis.T,
        anchor_embed / n_group - embed_here / n_group,
        precision=lax.Precision.HIGHEST,
    )
    embed_factor = lax.psum(partial_factor, ("group", "shard"))
    embed_grad = jnp.dot(embed_basis, embed_factor, precision=lax.Precision.HIGHEST)
    new_anchor_embed, new_momentum_embed = nesterov(
        anchor_embed, momentum_embed, anchor_embed - embed_grad
    )
    new_embed_rows = new_anchor_embed.astype(jnp.bfloat16)
    return (
        new_anchor[None],
        new_moment[None],
        new_rows[None],
        new_anchor_embed,
        new_momentum_embed,
        new_embed_rows[None],
    )


def solution(mesh):
    in_specs = (
        P("group", None, "shard", None),
        P("shard", None, None, "group"),
        P("shard", None, None, "group"),
        P(),
        P("group", "shard", None),
        P("shard", None),
        P("shard", None),
        P("shard", None),
    )
    out_specs = (
        P("shard", None, None, "group"),
        P("shard", None, None, "group"),
        P("group", None, "shard", None),
        P("shard", None),
        P("shard", None),
        P("group", "shard", None),
    )
    return jax.shard_map(
        on_device, mesh=mesh, in_specs=in_specs, out_specs=out_specs, check_vma=False
    )
```

profile of v0, /device:TPU:1, one launch (start us, length us, event | category | flops | bytes accessed | tf_op | source)
XLA Modules:
  0.0 419.5 jit_solution(13820363118626524760)
XLA Ops:
  8.0 0.0 copy-start
  8.0 0.0 reduce-scatter.2.cloned.1.call-start
  8.1 1.0 convert_reduce_fusion
  9.1 0.7 iota_compare_fusion.1
  9.8 0.1 fusion.4
  9.9 0.1 and_reduce_fusion
  10.0 0.1 reshape.127
  10.1 2.8 gather_fusion
  13.0 2.6 select_select_fusion
  15.5 0.6 copy.21
  16.1 65.2 %all_to_all.10 = bf16[2,64,8,2048]{3,2,0,1:T(8,128)(2,1)S(1)} all-to-all(bf16[2,64,8,2048]{3,2,0,1:T(8,128)(2,1)S(1)} %copy.21), channel_id=1, replica_groups=mesh['group'=2,'shard'=64] {'shard'}, dimensions={1} | all-to-all | bytes 8388608 | tf_op jit(solution)/shard_map/all_to_all | solution.py:57
  81.3 2.3 copy.26
  83.6 0.0 reduce-scatter.2.cloned.1.call-update
  83.7 0.0 all-gather.2.cloned.1.call-start
  83.7 0.2 dynamic-slice_reduce_fusion
  83.9 52.2 %reduce-scatter.2.cloned.1.call-done = bf16[2,512,1024]{2,1,0:T(8,128)(2,1)} async-done(((bf16[2,512,2048]{2,1,0:T(8,128)(2,1)}), bf16[2,512,1024]{2,1,0:T(8,128)(2,1)}) %reduce-scatter.2.cloned.1.call-update) | async-done | bytes 2097168 | tf_op jit(solution)/shard_map/reduce_scatter | solution.py:65
  136.1 9.8 %fusion.13 = (bf16[2,512,1024]{2,1,0:T(8,128)(2,1)}, f32[1,2,512,1024]{3,2,1,0:T(8,128)}, f32[1,2,512,1024]{3,2,1,0:T(8,128)}) fusion(f32[1,2,512,1024]{3,2,1,0:T(8,128)} %param.10, bf16[2,512,1024]{2,1,0:T(8,128)(2,1)} %reduce-scatter.2.cloned.1.call-done, f32[1,2,512,1024]{3,2,1,0:T(8,128)} %param.9, pred[2]{0:T(512)(128)(4,1)S(1)} %dynamic-slice_reduce_fusion), kind=kLoop, calls=%fused_computation.42 | loop fusion | flops 12582912 | bytes 20971522 | tf_op jit(solution)/shard_map/convert_element_type | solution.py:72
  145.9 0.0 all-gather.2.cloned.1.call-update
  146.0 60.4 %all-gather.2.cloned.1.call-done = bf16[2,512,2048]{2,1,0:T(8,128)(2,1)} async-done(((bf16[2,512,1024]{2,1,0:T(8,128)(2,1)}), bf16[2,512,2048]{2,1,0:T(8,128)(2,1)}) %all-gather.2.cloned.1.call-update) | async-done | bytes 4194320 | tf_op jit(solution)/shard_map/all_gather | solution.py:73
  206.3 4.7 %copy.23 = bf16[2,64,8,2048]{3,2,0,1:T(8,128)(2,1)} copy(bf16[2,64,8,2048]{3,2,1,0:T(8,128)(2,1)} %bitcast.70) | data formatting | bytes 8388608 | tf_op jit(solution)/shard_map/reshape | solution.py:74
  211.1 0.0 copy-start.2
  211.1 10.7 %all-to-all-start.1 = ((bf16[2,64,8,2048]{3,2,0,1:T(8,128)(2,1)}), bf16[2,64,8,2048]{3,2,0,1:T(8,128)(2,1)}, u32[]{:S(2)}, u32[]{:S(2)}) async-start(bf16[2,64,8,2048]{3,2,0,1:T(8,128)(2,1)} %copy.23), calls=%async_computation.2 | async-start | bytes 8388608 | tf_op jit(solution)/shard_map/all_to_all | solution.py:75
  221.8 0.0 all-reduce.2.cloned.1.call-start
  221.9 0.0 copy-done.1
  221.9 1.0 convolution_bitcast_fusion
  222.9 0.0 all-reduce.2.cloned.1.call-update
  222.9 175.3 %all-reduce.2.cloned.1.call-done = f32[64,512]{1,0:T(8,128)} async-done(((f32[64,512]{1,0:T(8,128)}), f32[64,512]{1,0:T(8,128)}) %all-reduce.2.cloned.1.call-update) | async-done | bytes 131088 | tf_op jit(solution)/shard_map/psum | solution.py:84
  398.2 1.7 convert_bitcast_fusion
  400.0 0.0 all-to-all-done.1
  400.0 4.7 %copy.24 = bf16[2,64,8,2048]{3,2,1,0:T(8,128)(2,1)} copy(bf16[2,64,8,2048]{3,2,0,1:T(8,128)(2,1)} %all-to-all-done.1) | data formatting | bytes 8388608 | tf_op jit(solution)/shard_map/all_to_all | solution.py:75
  404.7 4.2 gather_fusion.1
  408.9 3.2 bitcast_select_fusion.1
  (15 shorter events, 0.1 us)
Async XLA Ops:
  8.0 2.1 copy-start
  8.0 128.1 %reduce-scatter.2.cloned.1.call-start = ((), (), s32[]{:S(2)}) async-start(), calls=%async_computation.3 | async-start | bytes 6291456 | tf_op jit(solution)/shard_map/reduce_scatter | solution.py:65
  83.7 122.6 %all-gather.2.cloned.1.call-start = ((), (), s32[]{:S(2)}) async-start(), calls=%async_computation.4 | async-start | bytes 6291456 | tf_op jit(solution)/shard_map/all_gather | solution.py:73
  211.1 10.8 %copy-start.1 = (f32[12,512]{1,0:T(8,128)S(1)}, f32[12,512]{1,0:T(8,128)}, u32[]{:S(2)}) copy-start(f32[12,512]{1,0:T(8,128)} %param.13) | copy-start | bytes 73732
  211.1 10.8 %copy-start.3 = (f32[12,64]{1,0:T(8,128)S(1)}, f32[12,64]{1,0:T(8,128)}, u32[]{:S(2)}) copy-start(f32[12,64]{1,0:T(8,128)} %param.15) | copy-start | bytes 9220
  211.1 10.8 %copy-start.4 = (bf16[1,12,512]{2,1,0:T(8,128)(2,1)S(1)}, bf16[1,12,512]{2,1,0:T(8,128)(2,1)}, u32[]{:S(2)}) copy-start(bf16[1,12,512]{2,1,0:T(8,128)(2,1)} %param.12) | copy-start | bytes 36868
  211.1 11.8 %copy-start.5 = (s32[64]{0:T(128)S(1)}, s32[64]{0:T(128)}, u32[]{:S(2)}) copy-start(s32[64]{0:T(128)} %param.11) | copy-start | bytes 772
  211.1 187.2 %copy-start.2 = (f32[12,512]{1,0:T(8,128)S(1)}, f32[12,512]{1,0:T(8,128)}, u32[]{:S(2)}) copy-start(f32[12,512]{1,0:T(8,128)} %param.14) | copy-start | bytes 73732
  211.1 188.9 %all-to-all-start.1 = ((bf16[2,64,8,2048]{3,2,0,1:T(8,128)(2,1)}), bf16[2,64,8,2048]{3,2,0,1:T(8,128)(2,1)}, u32[]{:S(2)}, u32[]{:S(2)}) async-start(bf16[2,64,8,2048]{3,2,0,1:T(8,128)(2,1)} %copy.23), calls=%async_computation.2 | async-start | bytes 8388608 | tf_op jit(solution)/shard_map/all_to_all | solution.py:75
  221.8 176.4 %all-reduce.2.cloned.1.call-start = ((), (), s32[]{:S(2)}) async-start(), calls=%async_computation.5 | async-start | bytes 262144 | tf_op jit(solution)/shard_map/psum | solution.py:84
Sparse Core Ops, SparseCore 0:
  83.8 52.2 reduce-scatter.1
  146.1 60.1 all-gather.1
Sparse Core Ops, SparseCore 1:
  227.6 170.6 all-reduce.1
where the time goes:
time: 420 us
  waiting for transfers between devices  288 us (69%)
  blocking collectives  65.2 us (16%)
  local copies, waits for them, and re-layouts  19.7 us (5%)
  other arithmetic  17.5 us (4%)
  between operations  15.6 us (4%)
  starting transfers between devices  10.8 us (3%)
    psum x1, waiting for transfers between devices, on_device(): embed_factor = lax.psum(partial_factor, ('group', 'shard'))  175 us
    all_to_all x1, blocking collectives, on_device(): lax.all_to_all(jnp.where(send_used[:, :, None, None], picked, jnp.zeros((...  65.2 us
    all_gather x1, waiting for transfers between devices, on_device(): full_cols = lax.all_gather(new_half, 'group', axis=2, tiled=True)  60.4 us
    reduce_scatter x1, waiting for transfers between devices, on_device(): lax.psum_scatter(gathered.astype(jnp.float32).astype(jnp.bfloat16), 'grou...  52.2 us
    all_to_all x1, starting transfers between devices, on_device(): lax.all_to_all(split_rows, 'shard', split_axis=1, concat_axis=1, tiled=True)  10.7 us
    convert_element_type x1, other arithmetic, on_device(): new_half = new_anchor.astype(jnp.bfloat16)  9.8 us
  transfers between devices with their start and end apart: 4, of which 3 were waited for; matrix products, arithmetic and copies ran while one was open for 1% of the time, Pallas kernels for 0%

commit v1 on v0

--- a/solution.py
+++ b/solution.py
@@ -40,41 +40,32 @@
 ):
     local_rows = replica_weights[0]
     row_count = local_rows.shape[1]
-    width = local_rows.shape[2]
     devices = lax.axis_size("shard")
     n_group = lax.axis_size("group")
     capacity = anchor_slabs.shape[1]
     slot_index, slab_of, slot_used = slot_tables(slab_owner, devices, capacity)
     send_ids = slab_of.T.reshape(-1)
-    send_used = slot_used.T
     back_ids = slot_index * devices + slab_owner
     owner_here = lax.axis_index("shard")
     my_used = lax.dynamic_index_in_dim(slot_used, owner_here, 0, keepdims=False)
     anchor_here = anchor_slabs[0]
     moment_here = momentum_slabs[0]
-    picked = jnp.take(local_rows, send_ids, axis=0)
-    picked = picked.reshape(capacity, devices, local_rows.shape[1], local_rows.shape[2])
-    received = lax.all_to_all(
-        jnp.where(send_used[:, :, None, None], picked, jnp.zeros((), local_rows.dtype)),
-        "shard",
-        split_axis=1,
-        concat_axis=1,
-        tiled=True,
-    )
-    gathered = received.reshape(capacity, devices * received.shape[2], received.shape[3])
-    summed = lax.psum_scatter(
-        gathered.astype(jnp.float32).astype(jnp.bfloat16), "group", scatter_dimension=2, tiled=True
-    ).astype(jnp.float32)
+    summed_rows = lax.psum_scatter(local_rows, "group", scatter_dimension=2, tiled=True)
+    half = summed_rows.shape[2]
+    picked = jnp.take(summed_rows, send_ids, axis=0)
+    picked = picked.reshape(capacity, devices, row_count, half)
+    received = lax.all_to_all(picked, "shard", split_axis=1, concat_axis=1, tiled=True)
+    summed = received.reshape(capacity, devices * row_count, half).astype(jnp.float32)
     new_anchor, new_moment = nesterov(anchor_here, moment_here, summed / n_group)
     keep = my_used[:, None, None]
     new_anchor = jnp.where(keep, new_anchor, anchor_here)
     new_moment = jnp.where(keep, new_moment, moment_here)
     new_half = new_anchor.astype(jnp.bfloat16)
-    full_cols = lax.all_gather(new_half, "group", axis=2, tiled=True)
-    split_rows = full_cols.reshape(capacity, devices, row_count, width)
+    split_rows = new_half.reshape(capacity, devices, row_count, half)
     received = lax.all_to_all(split_rows, "shard", split_axis=1, concat_axis=1, tiled=True)
-    flat_rows = received.reshape(capacity * devices, received.shape[2], received.shape[3])
-    new_rows = jnp.take(flat_rows, back_ids, axis=0)
+    flat_rows = received.reshape(capacity * devices, row_count, half)
+    half_rows = jnp.take(flat_rows, back_ids, axis=0)
+    new_rows = lax.all_gather(half_rows, "group", axis=2, tiled=True)
     embed_here = replica_embed[0].astype(jnp.float32)
     partial_factor = jnp.dot(
         embed_basis.T,

time: 420 us -> 294 us (0.70)
  blocking collectives: 65.2 us -> 0 us
  waiting for transfers between devices: 288 us -> 231 us
  local copies, waits for them, and re-layouts: 19.7 us -> 13.8 us
  starting transfers between devices: 10.8 us -> 15.6 us
    all_to_all x1 -> x0, blocking collectives: 65.2 us -> none  [on_device(): lax.all_to_all(jnp.where(send_used[:, :, None, None], picked, jnp.zeros((...]
    all_gather x1, waiting for transfers between devices: 60.4 us -> 0.01 us  [on_device(): new_rows = lax.all_gather(half_rows, 'group', axis=2, tiled=True)]
    psum x1, waiting for transfers between devices: 175 us -> 133 us  [on_device(): embed_factor = lax.psum(partial_factor, ('group', 'shard'))]
    all_to_all x0 -> x1, waiting for transfers between devices: none -> 30.2 us  [on_device(): lax.all_to_all(picked, 'shard', split_axis=1, concat_axis=1, tiled=True)]
    all_to_all x1, waiting for transfers between devices: 0.01 us -> 29.3 us  [on_device(): lax.all_to_all(split_rows, 'shard', split_axis=1, concat_axis=1, tiled=True)]
    reduce_scatter x1, waiting for transfers between devices: 52.2 us -> 38 us  [on_device(): lax.psum_scatter(local_rows, 'group', scatter_dimension=2, tiled=True)]
    all_to_all x0 -> x1, starting transfers between devices: none -> 10.4 us  [on_device(): lax.all_to_all(picked, 'shard', split_axis=1, concat_axis=1, tiled=True)]
    all_to_all x1, starting transfers between devices: 10.7 us -> 5.13 us  [on_device(): lax.all_to_all(split_rows, 'shard', split_axis=1, concat_axis=1, tiled=True)]
  transfers between devices with their start and end apart: 4 -> 5, of which waited for: 3 -> 4; matrix products, arithmetic and copies ran while one was open for 1% -> 6% of each run, Pallas kernels for 0% -> 0%
where the time goes in v1:
time: 294 us
  waiting for transfers between devices  231 us (79%)
  starting transfers between devices  15.6 us (5%)
  between operations  15.6 us (5%)
  other arithmetic  15 us (5%)
  local copies, waits for them, and re-layouts  13.8 us (5%)
    psum x1, waiting for transfers between devices, on_device(): embed_factor = lax.psum(partial_factor, ('group', 'shard'))  133 us
    reduce_scatter x1, waiting for transfers between devices, on_device(): lax.psum_scatter(local_rows, 'group', scatter_dimension=2, tiled=True)  38 us
    all_to_all x1, waiting for transfers between devices, on_device(): lax.all_to_all(picked, 'shard', split_axis=1, concat_axis=1, tiled=True)  30.2 us
    all_to_all x1, waiting for transfers between devices, on_device(): lax.all_to_all(split_rows, 'shard', split_axis=1, concat_axis=1, tiled=True)  29.3 us
    all_to_all x1, starting transfers between devices, on_device(): lax.all_to_all(picked, 'shard', split_axis=1, concat_axis=1, tiled=True)  10.4 us
    select_n x1, other arithmetic, on_device(): new_moment = jnp.where(keep, new_moment, moment_here)  6.66 us
  transfers between devices with their start and end apart: 5, of which 4 were waited for; matrix products, arithmetic and copies ran while one was open for 6% of the time, Pallas kernels for 0%

profile of v1, /device:TPU:1, one launch (start us, length us, event | category | flops | bytes accessed | tf_op | source)
XLA Modules:
  0.0 293.8 jit_solution(6259343763254815098)
XLA Ops:
  8.0 0.0 copy-start
  8.0 0.0 reduce-scatter.2.cloned.1.call-start
  8.1 0.7 reduce-scatter.2.cloned.1.call-update
  8.7 0.9 convert_reduce_fusion
  9.7 0.7 iota_compare_fusion.1
  10.4 0.1 fusion.8
  10.5 0.1 reshape.136
  10.6 38.0 %reduce-scatter.2.cloned.1.call-done = bf16[64,8,1024]{2,1,0:T(8,128)(2,1)} async-done(((bf16[64,8,2048]{2,1,0:T(8,128)(2,1)}), bf16[64,8,1024]{2,1,0:T(8,128)(2,1)}) %reduce-scatter.2.cloned.1.call-update) | async-done | bytes 1048592 | tf_op jit(solution)/shard_map/reduce_scatter | solution.py:53
  48.7 1.9 gather_fusion
  50.6 0.3 broadcast_select_fusion
  50.8 1.5 copy.19
  52.4 10.4 %all-to-all-start = ((bf16[2,64,8,1024]{3,2,0,1:T(8,128)(2,1)}), bf16[2,64,8,1024]{3,2,0,1:T(8,128)(2,1)S(1)}, u32[]{:S(2)}, u32[]{:S(2)}) async-start(bf16[2,64,8,1024]{3,2,0,1:T(8,128)(2,1)} %copy.19), calls=%async_computation.1 | async-start | bytes 4194304 | tf_op jit(solution)/shard_map/all_to_all | solution.py:57
  62.8 0.1 and_reduce_fusion
  62.9 0.2 dynamic-slice_reduce_fusion
  63.1 30.2 %all-to-all-done = bf16[2,64,8,1024]{3,2,0,1:T(8,128)(2,1)S(1)} async-done(((bf16[2,64,8,1024]{3,2,0,1:T(8,128)(2,1)}), bf16[2,64,8,1024]{3,2,0,1:T(8,128)(2,1)S(1)}, u32[]{:S(2)}, u32[]{:S(2)}) %all-to-all-start) | async-done | bytes 2097184 | tf_op jit(solution)/shard_map/all_to_all | solution.py:57
  93.3 5.1 %fusion = bf16[2,64,8,1024]{3,2,1,0:T(8,128)(2,1)S(1)} fusion(f32[1,2,512,1024]{3,2,1,0:T(8,128)} %param.9, f32[1,2,512,1024]{3,2,1,0:T(8,128)} %param.10, pred[2]{0:T(512)(128)(4,1)S(1)} %dynamic-slice_reduce_fusion, bf16[2,64,8,1024]{3,2,0,1:T(8,128)(2,1)S(1)} %all-to-all-done), kind=kLoop, calls=%fused_computation.4 | loop fusion | flops 11534336 | bytes 12582914 | tf_op jit(solution)/shard_map/convert_element_type | solution.py:63
  98.3 0.0 copy-start.1
  98.4 1.6 copy.21
  99.9 5.1 %all-to-all-start.1 = ((bf16[2,64,8,1024]{3,2,0,1:T(8,128)(2,1)}), bf16[2,64,8,1024]{3,2,0,1:T(8,128)(2,1)}, u32[]{:S(2)}, u32[]{:S(2)}) async-start(bf16[2,64,8,1024]{3,2,0,1:T(8,128)(2,1)} %copy.21), calls=%async_computation.2 | async-start | bytes 4194304 | tf_op jit(solution)/shard_map/all_to_all | solution.py:65
  105.1 0.0 all-reduce.2.cloned.1.call-start
  105.1 1.0 convolution_bitcast_fusion
  106.1 0.0 all-reduce.2.cloned.1.call-update
  106.1 0.0 all-gather.2.cloned.1.call-start
  106.2 29.3 %all-to-all-done.1 = bf16[2,64,8,1024]{3,2,0,1:T(8,128)(2,1)} async-done(((bf16[2,64,8,1024]{3,2,0,1:T(8,128)(2,1)}), bf16[2,64,8,1024]{3,2,0,1:T(8,128)(2,1)}, u32[]{:S(2)}, u32[]{:S(2)}) %all-to-all-start.1) | async-done | bytes 2097184 | tf_op jit(solution)/shard_map/all_to_all | solution.py:65
  135.5 3.1 %copy.22 = bf16[2,64,8,1024]{3,2,1,0:T(8,128)(2,1)} copy(bf16[2,64,8,1024]{3,2,0,1:T(8,128)(2,1)} %all-to-all-done.1) | data formatting | bytes 4194304 | tf_op jit(solution)/shard_map/all_to_all | solution.py:65
  138.6 2.2 gather_fusion.1
  140.8 1.1 broadcast_select_fusion.1
  142.0 0.0 all-gather.2.cloned.1.call-update
  142.0 132.8 %all-reduce.2.cloned.1.call-done = f32[64,512]{1,0:T(8,128)} async-done(((f32[64,512]{1,0:T(8,128)}), f32[64,512]{1,0:T(8,128)}) %all-reduce.2.cloned.1.call-update) | async-done | bytes 131088 | tf_op jit(solution)/shard_map/psum | solution.py:75
  274.8 1.7 convert_bitcast_fusion
  276.5 6.7 %fusion.5 = (f32[1,2,512,1024]{3,2,1,0:T(8,128)}, f32[1,2,512,1024]{3,2,1,0:T(8,128)}) fusion(f32[1,2,512,1024]{3,2,1,0:T(8,128)} %param.10, f32[1,2,512,1024]{3,2,1,0:T(8,128)} %param.9, pred[2]{0:T(512)(128)(4,1)S(1)} %dynamic-slice_reduce_fusion, bf16[2,64,8,1024]{3,2,0,1:T(8,128)(2,1)S(1)} %all-to-all-done), kind=kLoop, calls=%fused_computation.13 | loop fusion | flops 11534336 | bytes 18874370 | tf_op jit(solution)/shard_map/jit(_where)/select_n | solution.py:62
  283.2 3.2 %copy.28 = bf16[1,64,8,2048]{3,2,1,0:T(8,128)(2,1)} copy(bf16[1,64,8,2048]{3,2,1,0:T(8,128)(2,1)} %bitcast.54) | data formatting | bytes 4194304
  (15 shorter events, 0.1 us)
Async XLA Ops:
  8.0 97.1 %copy-start = (f32[12,64]{1,0:T(8,128)S(1)}, f32[12,64]{1,0:T(8,128)}, u32[]{:S(2)}) copy-start(f32[12,64]{1,0:T(8,128)} %param.15) | copy-start | bytes 9220
  8.0 40.6 %reduce-scatter.2.cloned.1.call-start = ((), (), s32[]{:S(2)}) async-start(), calls=%async_computation.3 | async-start | bytes 3145728 | tf_op jit(solution)/shard_map/reduce_scatter | solution.py:53
  52.4 40.9 %all-to-all-start = ((bf16[2,64,8,1024]{3,2,0,1:T(8,128)(2,1)}), bf16[2,64,8,1024]{3,2,0,1:T(8,128)(2,1)S(1)}, u32[]{:S(2)}, u32[]{:S(2)}) async-start(bf16[2,64,8,1024]{3,2,0,1:T(8,128)(2,1)} %copy.19), calls=%async_computation.1 | async-start | bytes 4194304 | tf_op jit(solution)/shard_map/all_to_all | solution.py:57
  98.3 6.8 %copy-start.1 = (f32[12,512]{1,0:T(8,128)S(1)}, f32[12,512]{1,0:T(8,128)}, u32[]{:S(2)}) copy-start(f32[12,512]{1,0:T(8,128)} %param.13) | copy-start | bytes 73732
  98.3 6.8 %copy-start.3 = (bf16[1,12,512]{2,1,0:T(8,128)(2,1)S(1)}, bf16[1,12,512]{2,1,0:T(8,128)(2,1)}, u32[]{:S(2)}) copy-start(bf16[1,12,512]{2,1,0:T(8,128)(2,1)} %param.12) | copy-start | bytes 36868
  98.3 7.8 %copy-start.4 = (s32[64]{0:T(128)S(1)}, s32[64]{0:T(128)}, u32[]{:S(2)}) copy-start(s32[64]{0:T(128)} %param.11) | copy-start | bytes 772
  99.9 35.6 %all-to-all-start.1 = ((bf16[2,64,8,1024]{3,2,0,1:T(8,128)(2,1)}), bf16[2,64,8,1024]{3,2,0,1:T(8,128)(2,1)}, u32[]{:S(2)}, u32[]{:S(2)}) async-start(bf16[2,64,8,1024]{3,2,0,1:T(8,128)(2,1)} %copy.21), calls=%async_computation.2 | async-start | bytes 4194304 | tf_op jit(solution)/shard_map/all_to_all | solution.py:65
  105.1 169.7 %all-reduce.2.cloned.1.call-start = ((), (), s32[]{:S(2)}) async-start(), calls=%async_computation.5 | async-start | bytes 262144 | tf_op jit(solution)/shard_map/psum | solution.py:75
  106.1 177.0 %all-gather.2.cloned.1.call-start = ((), (), s32[]{:S(2)}) async-start(), calls=%async_computation.4 | async-start | bytes 3145728 | tf_op jit(solution)/shard_map/all_gather | solution.py:68
  106.2 168.5 %copy-start.2 = (f32[12,512]{1,0:T(8,128)S(1)}, f32[12,512]{1,0:T(8,128)}, u32[]{:S(2)}) copy-start(f32[12,512]{1,0:T(8,128)} %param.14) | copy-start | bytes 73732
Sparse Core Ops, SparseCore 0:
  11.2 37.4 reduce-scatter.1
  142.1 30.8 all-gather.1
Sparse Core Ops, SparseCore 1:
  110.9 163.8 all-reduce.1

commit v2 on v1

v2 whole, which is shorter than its diff:
```python
import functools

import jax
import jax.numpy as jnp
from jax import lax
from jax.experimental import pallas as pl
from jax.experimental.pallas import tpu as pltpu
from jax.sharding import PartitionSpec as P

OUTER_RATE = 0.7
MOMENTUM_COEF = 0.9
GRAD_COEF = OUTER_RATE * (1.0 + MOMENTUM_COEF)
MOMENT_COEF = OUTER_RATE * MOMENTUM_COEF * MOMENTUM_COEF
PLANES = 2
INNER = {64: 8, 8: 2}
CHUNKS = 4
UNROLL = 4
MESH = pl.DeviceIdType.MESH


def place(shard, inner):
    plane = lax.rem(lax.div(shard, inner), PLANES)
    spot = lax.div(shard, PLANES * inner) * inner + lax.rem(shard, inner)
    return plane, spot


def shard_of(spot, plane, inner):
    return lax.div(spot, inner) * (PLANES * inner) + plane * inner + lax.rem(spot, inner)


def loop(count, body):
    unroll = UNROLL if count % UNROLL == 0 else 1

    def step(i, carry):
        for u in range(unroll):
            body(i * unroll + u)
        return carry

    lax.fori_loop(0, count // unroll, step, 0)


def each(start, stop, body):
    def step(i, carry):
        body(i)
        return carry

    lax.fori_loop(start, stop, step, 0)


def route_kernel(sizes, tabs, xs, xo, q, part, n_out, nr_out, f_out, e_out, *scratch):
    shards, slabs, slots, ranks, inner, width = sizes
    chunks = CHUNKS
    spots = shards // PLANES
    (r, s, fc, cf, ys, qr, qc, qd, nn) = [scratch[i * chunks : (i + 1) * chunks] for i in range(9)]
    er, e1, ex, e2, *sems = scratch[9 * chunks :]
    (sa, ra, sc, rc, sq, rq, sd, rd, sf, sn, lo) = sems[:11]
    (rf, rn, se, re, sx, rx, sg, rg, le) = sems[11:]

    group = lax.axis_index("group")
    shard = lax.axis_index("shard")
    plane, spot = place(shard, inner)
    line, lane = lax.div(spot, inner), lax.rem(spot, inner)
    other = 1 - plane
    partner = (1 - group, shard)
    across = (1 - group, shard_of(spot, other, inner))
    corner = (group, shard_of(spot, other, inner))

    def peer(i):
        d = lax.rem(spot + i, spots)
        return d, (group, shard_of(d, plane, inner))

    def remote(src, dst, send, recv, device):
        return pltpu.make_async_remote_copy(
            src_ref=src, dst_ref=dst, send_sem=send, recv_sem=recv, device_id=device, device_id_type=MESH
        )

    def drain(ref, sem):
        pltpu.make_async_copy(ref, ref, sem).wait()

    off_fo, off_rk = 0, slots
    off_fc, off_fp = 2 * slots, 2 * slots + ranks
    off_in, off_ts = 2 * slots + 2 * ranks, 2 * slots + 2 * ranks + slabs

    barrier = pltpu.get_barrier_semaphore()

    def greet(i):
        pl.semaphore_signal(barrier, inc=1, device_id=peer(i)[1], device_id_type=MESH)

    each(1, spots, greet)
    for device in (partner, across, corner):
        pl.semaphore_signal(barrier, inc=1, device_id=device, device_id_type=MESH)
    pl.semaphore_wait(barrier, spots - 1 + 3)

    def cols(k):
        return pl.ds(k * width, width)

    for k in range(chunks):
        remote(xs.at[:, :, cols(k)], r[k], sa.at[k], ra.at[k], partner).start()

    def send_part(i):
        d, device = peer(i)
        remote(part.at[d], er.at[spot], se, re, device).start()

    each(1, spots, send_part)
    er[spot] = part[spot]

    for k in range(chunks):

        def send_q(i, k=k):
            d, device = peer(i)
            remote(
                q.at[:, lax.div(d, inner), :, lax.rem(d, inner), :, cols(k)], qr[k].at[spot], sq.at[k], rq.at[k], device
            ).start()

        each(1, spots, send_q)
        pltpu.make_async_copy(q.at[:, line, :, lane, :, cols(k)], qr[k].at[spot], lo.at[k]).start()

    def stage_sum(k):
        drain(r[k], ra.at[k])

        def add(t):
            both = xo[t, :, cols(k)].astype(jnp.float32) + r[k][t].astype(jnp.float32)
            s[k][t] = both.astype(jnp.bfloat16)

        loop(slabs, add)

        def pick_cross(i):
            fc[k][i] = s[k][tabs[off_fc + i]]

        loop(ranks, pick_cross)
        remote(fc[k], cf[k], sc.at[k], rc.at[k], across).start()

        def pick_own(j):
            ys[k][lax.div(j, 2), lax.rem(j, 2), plane] = s[k][tabs[off_fo + j]]

        loop(slots, pick_own)

    def stage_q(k):
        drain(qr[k].at[pl.ds(0, spots - 1)], rq.at[k])
        drain(qr[k].at[0], lo.at[k])

        def pick(i):
            j = tabs[off_fp + i]
            qc[k][i] = qr[k][lax.div(j, 2), lax.rem(j, 2), other]

        loop(ranks, pick)
        remote(qc[k], qd[k], sd.at[k], rd.at[k], across).start()

    def stage_route(k):
        drain(cf[k], rc.at[k])

        def pick(j):
            ys[k][lax.div(j, 2), lax.rem(j, 2), other] = cf[k][tabs[off_rk + j]]

        loop(slots, pick)

        def send(i):
            d, device = peer(i)
            remote(ys[k].at[d], f_out.at[:, line, :, lane, :, cols(k)], sf.at[k], rf.at[k], device).start()

        each(1, spots, send)
        pltpu.make_async_copy(ys[k].at[spot], f_out.at[:, line, :, lane, :, cols(k)], lo.at[chunks + k]).start()

    def stage_new(k):
        drain(qd[k], rd.at[k])

        def combine(t):
            own = tabs[off_in + t]
            where = tabs[off_ts + t]
            j = where * own
            here = qr[k][lax.div(j, 2), lax.rem(j, 2), plane]
            there = qd[k][where * (1 - own)]
            base = jnp.where(own == 1, here.astype(jnp.float32), there.astype(jnp.float32))
            new = base + (0.5 * GRAD_COEF) * s[k][t].astype(jnp.float32)
            nn[k][t] = new.astype(jnp.bfloat16)

        loop(slabs, combine)
        remote(nn[k], nr_out.at[:, :, cols(k)], sn.at[k], rn.at[k], partner).start()
        pltpu.make_async_copy(nn[k], n_out.at[:, :, cols(k)], lo.at[2 * chunks + k]).start()

    def factor_sum():
        drain(er.at[pl.ds(0, spots - 1)], re)
        e1[...] = jnp.sum(er[...], axis=0)
        at = PLANES * plane + group
        ex[at] = e1[...]
        for n, device in enumerate((partner, across, corner)):
            remote(e1, ex.at[at], sx.at[n], rx.at[n], device).start()

    def factor_send():
        for n in range(3):
            drain(e1, rx.at[n])
        e2[...] = jnp.sum(ex[...], axis=0)

        def send(i):
            remote(e2, e_out.at[spot], sg, rg, peer(i)[1]).start()

        each(1, spots, send)
        pltpu.make_async_copy(e2, e_out.at[spot], le).start()

    for k in range(chunks):
        stage_sum(k)
        stage_q(k)
        if k == 0:
            factor_sum()
        if k == 1:
            factor_send()
        if k >= 1:
            stage_route(k - 1)
            stage_new(k - 1)
    stage_route(chunks - 1)
    stage_new(chunks - 1)

    for k in range(chunks):
        some = qr[k].at[pl.ds(0, spots - 1)]
        drain(r[k], sa.at[k])
        drain(cf[k], sc.at[k])
        drain(qd[k], sd.at[k])
        drain(some, sq.at[k])
        drain(some, sf.at[k])
        drain(nn[k], sn.at[k])
        drain(qr[k].at[0], lo.at[chunks + k])
        drain(nn[k], lo.at[2 * chunks + k])
        drain(some, rf.at[k])
        drain(nn[k], rn.at[k])
    for n in range(3):
        drain(e1, sx.at[n])
    drain(er.at[pl.ds(0, spots - 1)], se)
    drain(er.at[pl.ds(0, spots - 1)], sg)
    drain(er.at[pl.ds(0, spots - 1)], rg)
    drain(e2, le)


def route(tabs, xs, xo, q, part):
    slabs, rows, half = xs.shape
    slots_dev, lines, _, inner, _, _ = q.shape
    shards = lines * PLANES * inner
    spots = shards // PLANES
    slots = spots * slots_dev
    ranks = slabs * 3 // 4
    width = half // CHUNKS
    vmem = lambda *shape: [pltpu.VMEM(shape, jnp.bfloat16)] * CHUNKS
    sem = pltpu.SemaphoreType.DMA
    scratch = (
        vmem(slabs, rows, width)
        + vmem(slabs, rows, width)
        + vmem(ranks, rows, width)
        + vmem(ranks, rows, width)
        + vmem(spots, slots_dev, PLANES, rows, width)
        + vmem(spots, slots_dev, PLANES, rows, width)
        + vmem(ranks, rows, width)
        + vmem(ranks, rows, width)
        + vmem(slabs, rows, width)
        + [pltpu.VMEM((spots, 8, 128), jnp.float32)]
        + [pltpu.VMEM((8, 128), jnp.float32)]
        + [pltpu.VMEM((4, 8, 128), jnp.float32)]
        + [pltpu.VMEM((8, 128), jnp.float32)]
        + [sem((CHUNKS,))] * 10
        + [sem((3 * CHUNKS,))]
        + [sem((CHUNKS,)), sem((CHUNKS,)), sem(()), sem(()), sem((3,)), sem((3,)), sem(()), sem(()), sem(())]
    )
    vm = pl.BlockSpec(memory_space=pltpu.VMEM)
    anyspace = pl.BlockSpec(memory_space=pl.ANY)
    bf16 = jnp.bfloat16
    return pl.pallas_call(
        functools.partial(route_kernel, (shards, slabs, slots, ranks, inner, width)),
        out_shape=(
            jax.ShapeDtypeStruct(xs.shape, bf16),
            jax.ShapeDtypeStruct(xs.shape, bf16),
            jax.ShapeDtypeStruct(q.shape, bf16),
            jax.ShapeDtypeStruct((spots, 8, 128), jnp.float32),
        ),
        in_specs=[pl.BlockSpec(memory_space=pltpu.SMEM), vm, vm, vm, vm],
        out_specs=(anyspace, anyspace, anyspace, anyspace),
        scratch_shapes=scratch,
        compiler_params=pltpu.CompilerParams(collective_id=0, has_side_effects=True),
    )(tabs, xs, xo, q, part)


def tables(slab_owner, shards, inner, capacity, plane_here, spot_here):
    slabs = slab_owner.shape[0]
    slots = shards // PLANES * capacity
    ranks = slabs * 3 // 4
    ids = jnp.arange(slabs, dtype=jnp.int32)
    plane, spot = place(slab_owner, inner)
    earlier = ids[None, :] < ids[:, None]
    count = lambda mask: jnp.sum((mask & earlier).astype(jnp.int32), axis=1)
    slot = spot * capacity + count(slab_owner[:, None] == slab_owner[None, :])
    rank = count(plane[:, None] == plane[None, :])
    mine = plane == plane_here
    pick = lambda hit, value: jnp.sum(jnp.where(hit, value[None, :], 0), axis=1)
    at_slot = mine[None, :] & (slot[None, :] == jnp.arange(slots, dtype=jnp.int32)[:, None])
    at_rank = rank[None, :] == jnp.arange(ranks, dtype=jnp.int32)[:, None]
    tabs = jnp.concatenate(
        [
            pick(at_slot, ids),
            pick(at_slot, rank),
            pick(at_rank & ~mine[None, :], ids),
            pick(at_rank & mine[None, :], slot),
            mine.astype(jnp.int32),
            jnp.where(mine, slot, rank),
        ]
    )
    here = spot_here * capacity + jnp.arange(capacity, dtype=jnp.int32)
    used = jnp.any(mine[None, :] & (slot[None, :] == here[:, None]), axis=1)
    return tabs, mine, used


def nesterov(anchor_value, moment, mean_value):
    outer_grad = anchor_value - mean_value
    new_moment = MOMENTUM_COEF * moment + outer_grad
    new_anchor = anchor_value - OUTER_RATE * (outer_grad + MOMENTUM_COEF * new_moment)
    return (new_anchor, new_moment)


def on_device(
    replica_weights,
    anchor_slabs,
    momentum_slabs,
    slab_owner,
    replica_embed,
    anchor_embed,
    momentum_embed,
    embed_basis,
):
    rows = replica_weights[0]
    slabs, row_count, width = rows.shape
    half = width // 2
    shards = lax.axis_size("shard")
    n_group = lax.axis_size("group")
    inner = INNER[shards]
    lines = shards // PLANES // inner
    capacity = anchor_slabs.shape[1]
    anchor, moment = anchor_slabs[0], momentum_slabs[0]
    group = lax.axis_index("group")
    plane_here, spot_here = place(lax.axis_index("shard"), inner)
    tabs, mine, used = tables(slab_owner, shards, inner, capacity, plane_here, spot_here)

    keep_left = (mine == (group == 0))[:, None, None]
    left, right = rows[:, :, :half], rows[:, :, half:]
    xo = jnp.where(keep_left, left, right)
    xs = jnp.where(keep_left, right, left)
    q = ((1.0 - GRAD_COEF) * anchor - MOMENT_COEF * moment).astype(jnp.bfloat16)
    q = q.reshape(capacity, lines, PLANES, inner, row_count, half)

    embed_here = replica_embed[0].astype(jnp.float32)
    partial_factor = jnp.dot(
        embed_basis.T,
        anchor_embed / n_group - embed_here / n_group,
        precision=lax.Precision.HIGHEST,
    )
    part = partial_factor.reshape(shards // PLANES, 8, 128)

    near, far, sums, factor = route(tabs, xs, xo, q, part)

    new_rows = jnp.concatenate([jnp.where(keep_left, near, far), jnp.where(keep_left, far, near)], axis=2)
    summed = sums.reshape(anchor.shape).astype(jnp.float32)
    new_anchor, new_moment = nesterov(anchor, moment, summed / n_group)
    keep = used[:, None, None]
    new_anchor = jnp.where(keep, new_anchor, anchor)
    new_moment = jnp.where(keep, new_moment, moment)

    embed_factor = factor.reshape(partial_factor.shape)
    embed_grad = jnp.dot(embed_basis, embed_factor, precision=lax.Precision.HIGHEST)
    new_anchor_embed, new_momentum_embed = nesterov(
        anchor_embed, momentum_embed, anchor_embed - embed_grad
    )
    new_embed_rows = new_anchor_embed.astype(jnp.bfloat16)
    return (
        new_anchor[None],
        new_moment[None],
        new_rows[None],
        new_anchor_embed,
        new_momentum_embed,
        new_embed_rows[None],
    )


def solution(mesh):
    in_specs = (
        P("group", None, "shard", None),
        P("shard", None, None, "group"),
        P("shard", None, None, "group"),
        P(),
        P("group", "shard", None),
        P("shard", None),
        P("shard", None),
        P("shard", None),
    )
    out_specs = (
        P("shard", None, None, "group"),
        P("shard", None, None, "group"),
        P("group", None, "shard", None),
        P("shard", None),
        P("shard", None),
        P("group", "shard", None),
    )
    return jax.shard_map(
        on_device, mesh=mesh, in_specs=in_specs, out_specs=out_specs, check_vma=False
    )
```

time: 294 us -> 90.5 us (0.31)
  waiting for transfers between devices: 231 us -> 0 us
  Pallas kernels: 0 us -> 63.6 us
  starting transfers between devices: 15.6 us -> 0 us
  between operations: 15.6 us -> 0.75 us
  local copies, waits for them, and re-layouts: 13.8 us -> 4.51 us
  other arithmetic: 15 us -> 19.4 us
    psum x1 -> x0, waiting for transfers between devices: 133 us -> none  [on_device(): embed_factor = lax.psum(partial_factor, ('group', 'shard'))]
    pallas_call x0 -> x1, Pallas kernels: none -> 63.6 us  [route(): pl.pallas_call(functools.partial(route_kernel, (shards, slabs, slots, ran...]
    all_to_all x2 -> x0, waiting for transfers between devices: 59.4 us -> none  [the longest x1 30.2 us: on_device(): lax.all_to_all(picked, 'shard', split_axis=1, concat_axis=1, tiled=True)]
    reduce_scatter x1 -> x0, waiting for transfers between devices: 38 us -> none  [on_device(): lax.psum_scatter(local_rows, 'group', scatter_dimension=2, tiled=True)]
    all_to_all x2 -> x0, starting transfers between devices: 15.5 us -> none  [the longest x1 10.4 us: on_device(): lax.all_to_all(picked, 'shard', split_axis=1, concat_axis=1, tiled=True)]
    gather x2 -> x0, local copies, waits for them, and re-layouts: 4.11 us -> none  [the longest x1 2.2 us: on_device(): half_rows = jnp.take(flat_rows, back_ids, axis=0)]
    all_to_all x1 -> x0, local copies, waits for them, and re-layouts: 3.11 us -> none  [on_device(): lax.all_to_all(split_rows, 'shard', split_axis=1, concat_axis=1, tiled=True)]
    convert_element_type x1 -> x2, other arithmetic: 5.06 us -> 6.15 us  [the longest x1 6.14 us: on_device(): q = ((1.0 - GRAD_COEF) * anchor - MOMENT_COEF * moment).astype(jnp.bfloat16)]
  transfers between devices with their start and end apart: 5 -> 0, of which waited for: 4 -> 0; matrix products, arithmetic and copies ran while one was open for 6% -> 0% of each run, Pallas kernels for 0% -> 0%
where the time goes in v2:
time: 90.5 us; the launch traced here: 90.2 us
  Pallas kernels  63.6 us (70%)
  other arithmetic  19.4 us (21%)
  local copies, waits for them, and re-layouts  4.51 us (5%)
  matrix products  1.91 us (2%)
    pallas_call x1, Pallas kernels, route(): pl.pallas_call(functools.partial(route_kernel, (shards, slabs, slots, ran...  63.6 us
    convert_element_type x1, other arithmetic, on_device(): q = ((1.0 - GRAD_COEF) * anchor - MOMENT_COEF * moment).astype(jnp.bfloat16)  6.14 us
    select_n x1, other arithmetic, on_device(): new_moment = jnp.where(keep, new_moment, moment)  5.08 us
    unnamed x14, local copies, waits for them, and re-layouts  2.25 us
    select_n x1, other arithmetic, on_device(): jnp.where(keep_left, near, far)  1.89 us

profile of v2, /device:TPU:1, one launch (start us, length us, event | category | flops | bytes accessed | tf_op | source)
XLA Modules:
  0.0 90.2 jit_solution(17855860707953512746)
XLA Ops:
  0.6 0.0 copy-start
  0.7 0.7 broadcast_compare_fusion
  1.4 0.9 %convert_reduce_fusion = (s32[64]{0:T(128)S(1)}, s32[64]{0:T(128)S(1)}) fusion(s32[64]{0:T(128)S(1)} %get-tuple-element.23, s32[64]{0:T(128)} %param.11), kind=kLoop, calls=%fused_computation.21 | loop fusion | flops 36736 | bytes 1024 | tf_op jit(solution)/shard_map/reduce_sum | solution.py:286
  2.3 0.7 fusion.17
  2.9 0.2 and_reduce_fusion
  3.1 0.1 select_reduce_fusion
  3.3 0.1 select_reduce_fusion.2
  3.4 0.7 concatenate.6.tabs
  4.0 0.0 copy-done
  4.1 1.1 %convolution_bitcast_fusion = f32[64,512]{1,0:T(8,128)S(1)} fusion(f32[12,64]{1,0:T(8,128)S(1)} %copy-done, bf16[1,12,512]{2,1,0:T(8,128)(2,1)} %param.12, f32[12,512]{1,0:T(8,128)} %param.13), kind=kOutput, calls=%fused_computation.6 | convolution fusion | flops 4743168 | bytes 171008 | tf_op jit(solution)/shard_map/dot_general | solution.py:346
  5.1 0.7 reshape.63.part
  5.8 0.0 copy-start.4
  5.8 6.1 %subtract_convert_fusion = bf16[1,2,512,1024]{3,2,1,0:T(8,128)(2,1)} fusion(f32[1,2,512,1024]{3,2,1,0:T(8,128)} %param.10, f32[1,2,512,1024]{3,2,1,0:T(8,128)} %param.9), kind=kLoop, calls=%fused_computation.4 | loop fusion | flops 4194304 | bytes 10485760 | tf_op jit(solution)/shard_map/convert_element_type | solution.py:342
  11.9 0.0 copy-done.4
  11.9 0.0 copy-start.5
  11.9 0.0 copy-start.6
  11.9 1.5 %broadcast_select_fusion.2 = (bf16[64,8,1024]{2,1,0:T(8,128)(2,1)}, bf16[64,8,1024]{2,1,0:T(8,128)(2,1)}) fusion(pred[64]{0:T(512)(128)(4,1)S(1)} %get-tuple-element.21, bf16[64,8,2048]{2,1,0:T(8,128)(2,1)S(1)} %bitcast.25), kind=kLoop, calls=%fused_computation.12 | loop fusion | flops 1048576 | bytes 4194368 | tf_op jit(solution)/shard_map/jit(_where)/select_n | solution.py:340
  13.5 63.6 %shard_map.139 = (bf16[64,8,1024]{2,1,0:T(8,128)(2,1)}, bf16[64,8,1024]{2,1,0:T(8,128)(2,1)}, bf16[2,4,2,8,8,1024]{5,4,3,2,1,0:T(8,128)(2,1)}, f32[32,8,128]{2,1,0:T(8,128)}) custom-call(s32[352]{0:T(512)} %concatenate.6.tabs, bf16[64,8,1024]{2,1,0:T(8,128)(2,1)} %get-tuple-element.31.xs, bf16[64,8,1024]{2,1,0:T(8,128)(2,1)} %get-tuple-element.30.xo, ...), custom_call_target="tpu_custom_call" | custom-call | tf_op jit(solution)/shard_map/pallas_call | solution.py:264
  77.1 0.9 %reshape.64 = f32[64,512]{1,0:T(8,128)S(1)} reshape(f32[32,8,128]{2,1,0:T(8,128)} %get-tuple-element.13) | data formatting | bytes 262144 | tf_op jit(solution)/shard_map/reshape | solution.py:362
  78.0 0.0 copy-done.5
  78.0 0.0 copy-done.6
  78.0 0.8 convert_bitcast_fusion
  78.9 0.0 copy-start.3
  78.9 1.9 %broadcast_select_fusion.1 = (bf16[64,8,1024]{2,1,0:T(8,128)(2,1)S(1)}, bf16[64,8,1024]{2,1,0:T(8,128)(2,1)S(1)}) fusion(bf16[64,8,1024]{2,1,0:T(8,128)(2,1)} %get-tuple-element.11, bf16[64,8,1024]{2,1,0:T(8,128)(2,1)} %get-tuple-element.12, pred[64]{0:T(512)(128)(4,1)S(1)} %get-tuple-element.21), kind=kLoop, calls=%fused_computation.11 | loop fusion | flops 1048576 | bytes 4194368 | tf_op jit(solution)/shard_map/jit(_where)/select_n | solution.py:355
  80.8 0.0 copy-start.2
  80.8 1.5 %maximum_bitcast_fusion = bf16[1,64,8,2048]{3,2,1,0:T(8,128)(2,1)} fusion(bf16[64,8,1024]{2,1,0:T(8,128)(2,1)S(1)} %get-tuple-element.29, bf16[64,8,1024]{2,1,0:T(8,128)(2,1)S(1)} %get-tuple-element.28), kind=kLoop, calls=%fused_computation.5 | loop fusion | flops 4194304 | bytes 4194304 | tf_op jit(solution)/shard_map/broadcast_in_dim | solution.py:371
  82.3 0.0 copy-done.3
  82.3 0.0 copy-start.1
  82.3 0.6 convert_multiply_fusion
  82.9 0.9 %copy-done.2 = f32[1,2,512,1024]{3,2,1,0:T(8,128)S(1)} copy-done((f32[1,2,512,1024]{3,2,1,0:T(8,128)S(1)}, f32[1,2,512,1024]{3,2,1,0:T(8,128)}, u32[]{:S(2)}) %copy-start.2) | copy-done | bytes 4194328
  83.8 1.3 %copy-done.1 = f32[1,2,512,1024]{3,2,1,0:T(8,128)S(1)} copy-done((f32[1,2,512,1024]{3,2,1,0:T(8,128)S(1)}, f32[1,2,512,1024]{3,2,1,0:T(8,128)}, u32[]{:S(2)}) %copy-start.1) | copy-done | bytes 4194328
  85.1 5.1 %fusion = (f32[1,2,512,1024]{3,2,1,0:T(8,128)}, f32[1,2,512,1024]{3,2,1,0:T(8,128)}) fusion(f32[1,2,512,1024]{3,2,1,0:T(8,128)S(1)} %copy-done.1, f32[1,2,512,1024]{3,2,1,0:T(8,128)S(1)} %copy-done.2, f32[1,2,512,1024]{3,2,1,0:T(8,128)S(1)} %bitcast.23, pred[2]{0:T(512)(128)(4,1)S(1)} %and_reduce_fusion), kind=kLoop, calls=%fused_computation.2 | loop fusion | flops 9437184 | bytes 20971522 | tf_op jit(solution)/shard_map/jit(_where)/select_n | solution.py:360
  (2 shorter events, 0.0 us)
Async XLA Ops:
  0.6 3.4 %copy-start = (f32[12,64]{1,0:T(8,128)S(1)}, f32[12,64]{1,0:T(8,128)}, u32[]{:S(2)}) copy-start(f32[12,64]{1,0:T(8,128)} %param.15) | copy-start | bytes 9220
  5.8 6.1 %copy-start.4 = (bf16[1,64,8,2048]{3,2,1,0:T(8,128)(2,1)S(1)}, bf16[1,64,8,2048]{3,2,1,0:T(8,128)(2,1)}, u32[]{:S(2)}) copy-start(bf16[1,64,8,2048]{3,2,1,0:T(8,128)(2,1)} %param.8) | copy-start | bytes 6291460
  11.9 66.1 %copy-start.5 = (f32[12,512]{1,0:T(8,128)S(1)}, f32[12,512]{1,0:T(8,128)}, u32[]{:S(2)}) copy-start(f32[12,512]{1,0:T(8,128)} %param.13) | copy-start | bytes 73732
  11.9 66.1 %copy-start.6 = (f32[12,512]{1,0:T(8,128)S(1)}, f32[12,512]{1,0:T(8,128)}, u32[]{:S(2)}) copy-start(f32[12,512]{1,0:T(8,128)} %param.14) | copy-start | bytes 73732
  78.9 3.4 %copy-start.3 = (bf16[2,4,2,8,8,1024]{5,4,3,2,1,0:T(8,128)(2,1)S(1)}, bf16[2,4,2,8,8,1024]{5,4,3,2,1,0:T(8,128)(2,1)}, u32[]{:S(2)}) copy-start(bf16[2,4,2,8,8,1024]{5,4,3,2,1,0:T(8,128)(2,1)} %get-tuple-element.10) | copy-start | bytes 6291460
  80.8 3.0 %copy-start.2 = (f32[1,2,512,1024]{3,2,1,0:T(8,128)S(1)}, f32[1,2,512,1024]{3,2,1,0:T(8,128)}, u32[]{:S(2)}) copy-start(f32[1,2,512,1024]{3,2,1,0:T(8,128)} %param.9) | copy-start | bytes 12582916
  82.3 2.8 %copy-start.1 = (f32[1,2,512,1024]{3,2,1,0:T(8,128)S(1)}, f32[1,2,512,1024]{3,2,1,0:T(8,128)}, u32[]{:S(2)}) copy-start(f32[1,2,512,1024]{3,2,1,0:T(8,128)} %param.10) | copy-start | bytes 12582916

commit v3 on v2

v3 whole, which is shorter than its diff:
```python
import functools

import jax
import jax.numpy as jnp
from jax import lax
from jax.experimental import pallas as pl
from jax.experimental.pallas import tpu as pltpu
from jax.sharding import PartitionSpec as P

OUTER_RATE = 0.7
MOMENTUM_COEF = 0.9
GRAD_COEF = OUTER_RATE * (1.0 + MOMENTUM_COEF)
MOMENT_COEF = OUTER_RATE * MOMENTUM_COEF * MOMENTUM_COEF
PLANES = 2
INNER = {64: 8, 8: 2}
CHUNKS = 4
UNROLL = 4
MESH = pl.DeviceIdType.MESH


def place(shard, inner):
    plane = lax.rem(lax.div(shard, inner), PLANES)
    spot = lax.div(shard, PLANES * inner) * inner + lax.rem(shard, inner)
    return plane, spot


def shard_of(spot, plane, inner):
    return lax.div(spot, inner) * (PLANES * inner) + plane * inner + lax.rem(spot, inner)


def loop(count, body):
    unroll = UNROLL if count % UNROLL == 0 else 1

    def step(i, carry):
        for u in range(unroll):
            body(i * unroll + u)
        return carry

    lax.fori_loop(0, count // unroll, step, 0)


def each(start, stop, body):
    def step(i, carry):
        body(i)
        return carry

    lax.fori_loop(start, stop, step, 0)


def route_kernel(sizes, tabs, x, a, m, basis, embed, anchor_embed, na, nm, w_out, e_out, *scratch):
    shards, slabs, slots, ranks, inner, width = sizes
    chunks = CHUNKS
    spots = shards // PLANES
    capacity = slots // spots
    half = width * chunks
    bf16, f32 = jnp.bfloat16, jnp.float32
    (xl, xr, xs, xo, r, s, fc, cf, ys, fr, qb, qr, qc, qd, nn, nr) = [
        scratch[i * chunks : (i + 1) * chunks] for i in range(16)
    ]
    part, er, e1, ex, e2, *sems = scratch[16 * chunks :]
    (sa, ra, sc, rc, sq, rq, sd, rd, sf, rf, sn, rn, lx, ly, la, lm, lq, lf) = sems[:18]
    (se, re, sx, rx, sg, rg, le) = sems[18:]

    group = lax.axis_index("group")
    shard = lax.axis_index("shard")
    plane, spot = place(shard, inner)
    line, lane = lax.div(spot, inner), lax.rem(spot, inner)
    other = 1 - plane
    partner = (1 - group, shard)
    across = (1 - group, shard_of(spot, other, inner))
    corner = (group, shard_of(spot, other, inner))

    def peer(i):
        d = lax.rem(spot + i, spots)
        return d, (group, shard_of(d, plane, inner))

    def remote(src, dst, send, recv, device):
        return pltpu.make_async_remote_copy(
            src_ref=src, dst_ref=dst, send_sem=send, recv_sem=recv, device_id=device, device_id_type=MESH
        )

    def drain(ref, sem):
        pltpu.make_async_copy(ref, ref, sem).wait()

    off_fo, off_rk = 0, slots
    off_fc, off_fp = 2 * slots, 2 * slots + ranks
    off_in, off_ts = 2 * slots + 2 * ranks, 2 * slots + 2 * ranks + slabs
    off_used = off_ts + slabs

    def cols(k):
        return pl.ds(k * width, width)

    def right(k):
        return pl.ds(half + k * width, width)

    for k in range(chunks):
        pltpu.make_async_copy(x.at[:, :, cols(k)], xl[k], lx.at[k]).start()
        pltpu.make_async_copy(x.at[:, :, right(k)], xr[k], ly.at[k]).start()
        pltpu.make_async_copy(a.at[:, :, :, cols(k)], na.at[:, :, :, cols(k)], la.at[k]).start()
        pltpu.make_async_copy(m.at[:, :, :, cols(k)], nm.at[:, :, :, cols(k)], lm.at[k]).start()

    barrier = pltpu.get_barrier_semaphore()

    def greet(i):
        pl.semaphore_signal(barrier, inc=1, device_id=peer(i)[1], device_id_type=MESH)

    each(1, spots, greet)
    for device in (partner, across, corner):
        pl.semaphore_signal(barrier, inc=1, device_id=device, device_id_type=MESH)
    pl.semaphore_wait(barrier, spots - 1 + 3)

    def is_left(t):
        return lax.rem(tabs[off_in + t] + group, 2) == 1

    def start_x(k):
        drain(xl[k], lx.at[k])
        drain(xr[k], ly.at[k])

        def split(t):
            left = is_left(t)
            one, two = xl[k][t], xr[k][t]
            xs[k][t] = jnp.where(left, two, one)
            xo[k][t] = jnp.where(left, one, two)

        loop(slabs, split)
        remote(xs[k], r[k], sa.at[k], ra.at[k], partner).start()

    def start_q(k):
        drain(na.at[:, :, :, cols(k)], la.at[k])
        drain(nm.at[:, :, :, cols(k)], lm.at[k])

        def base(n):
            z, b, i = lax.div(n, PLANES * inner), lax.rem(lax.div(n, inner), PLANES), lax.rem(n, inner)
            for c in range(capacity):
                value = (1.0 - GRAD_COEF) * na[c, n, :, cols(k)] - MOMENT_COEF * nm[c, n, :, cols(k)]
                qb[k][c, z, b, i] = value.astype(bf16)

        loop(shards, base)

        def send_q(i):
            d, device = peer(i)
            remote(
                qb[k].at[:, lax.div(d, inner), :, lax.rem(d, inner)], qr[k].at[spot], sq.at[k], rq.at[k], device
            ).start()

        each(1, spots, send_q)
        pltpu.make_async_copy(qb[k].at[:, line, :, lane], qr[k].at[spot], lq.at[k]).start()

    def tile(ref, d):
        per = ref.shape[1] // 128
        return ref.at[pl.ds(lax.div(d, per) * 8, 8), pl.ds(pl.multiple_of(lax.rem(d, per) * 128, 128), 128)]

    def factor_start():
        diff = 0.5 * anchor_embed[...] - 0.5 * embed[...].astype(f32)
        part[...] = lax.dot_general(
            basis[...], diff, (((0,), (0,)), ((), ())), precision=lax.Precision.HIGHEST, preferred_element_type=f32
        )

        def send_part(i):
            d, device = peer(i)
            remote(tile(part, d), er.at[spot], se, re, device).start()

        each(1, spots, send_part)
        er[spot] = tile(part, spot)[...]

    def stage_sum(k):
        drain(r[k], ra.at[k])

        def add(t):
            both = xo[k][t].astype(f32) + r[k][t].astype(f32)
            s[k][t] = both.astype(bf16)

        loop(slabs, add)

        def pick_cross(i):
            fc[k][i] = s[k][tabs[off_fc + i]]

        loop(ranks, pick_cross)
        remote(fc[k], cf[k], sc.at[k], rc.at[k], across).start()

        def pick_own(j):
            ys[k][lax.div(j, capacity), lax.rem(j, capacity), plane] = s[k][tabs[off_fo + j]]

        loop(slots, pick_own)

    def stage_q(k):
        drain(qr[k].at[pl.ds(0, spots - 1)], rq.at[k])
        drain(qr[k].at[0], lq.at[k])

        def pick(i):
            j = tabs[off_fp + i]
            qc[k][i] = qr[k][lax.div(j, capacity), lax.rem(j, capacity), other]

        loop(ranks, pick)
        remote(qc[k], qd[k], sd.at[k], rd.at[k], across).start()

    def stage_route(k):
        drain(cf[k], rc.at[k])

        def pick(j):
            ys[k][lax.div(j, capacity), lax.rem(j, capacity), other] = cf[k][tabs[off_rk + j]]

        loop(slots, pick)

        def send(i):
            d, device = peer(i)
            remote(ys[k].at[d], fr[k].at[:, line, :, lane], sf.at[k], rf.at[k], device).start()

        each(1, spots, send)
        pltpu.make_async_copy(ys[k].at[spot], fr[k].at[:, line, :, lane], lf.at[k]).start()

    def stage_new(k):
        drain(qd[k], rd.at[k])

        def combine(t):
            own = tabs[off_in + t]
            where = tabs[off_ts + t]
            j = where * own
            here = qr[k][lax.div(j, capacity), lax.rem(j, capacity), plane]
            there = qd[k][where * (1 - own)]
            base = jnp.where(own == 1, here.astype(f32), there.astype(f32))
            new = base + (0.5 * GRAD_COEF) * s[k][t].astype(f32)
            nn[k][t] = new.astype(bf16)

        loop(slabs, combine)
        remote(nn[k], nr[k], sn.at[k], rn.at[k], partner).start()

    def finish_owned(k):
        drain(qr[k].at[pl.ds(0, spots - 1)], rf.at[k])
        drain(qr[k].at[0], lf.at[k])

        def step(n):
            z, b, i = lax.div(n, PLANES * inner), lax.rem(lax.div(n, inner), PLANES), lax.rem(n, inner)
            for c in range(capacity):
                used = tabs[off_used + c] == 1
                anchor, moment = na[c, n, :, cols(k)], nm[c, n, :, cols(k)]
                new_anchor, new_moment = nesterov(anchor, moment, 0.5 * fr[k][c, z, b, i].astype(f32))
                na[c, n, :, cols(k)] = jnp.where(used, new_anchor, anchor)
                nm[c, n, :, cols(k)] = jnp.where(used, new_moment, moment)

        loop(shards, step)

    def finish_weights(k):
        drain(nr[k], rn.at[k])

        def merge(t):
            left = is_left(t)
            near, far = nn[k][t], nr[k][t]
            w_out[t, :, cols(k)] = jnp.where(left, near, far)
            w_out[t, :, right(k)] = jnp.where(left, far, near)

        loop(slabs, merge)

    def factor_sum():
        drain(er.at[pl.ds(0, spots - 1)], re)
        e1[...] = jnp.sum(er[...], axis=0)
        at = PLANES * plane + group
        ex[at] = e1[...]
        for n, device in enumerate((partner, across, corner)):
            remote(e1, ex.at[at], sx.at[n], rx.at[n], device).start()

    def factor_send():
        for n in range(3):
            drain(e1, rx.at[n])
        e2[...] = jnp.sum(ex[...], axis=0)

        def send(i):
            remote(e2, tile(e_out, spot), sg, rg, peer(i)[1]).start()

        each(1, spots, send)
        pltpu.make_async_copy(e2, tile(e_out, spot), le).start()

    for k in range(chunks):
        start_x(k)
        start_q(k)
        if k == 0:
            factor_start()
    for k in range(chunks):
        stage_sum(k)
        stage_q(k)
        if k == 0:
            factor_sum()
        if k == 1:
            factor_send()
        if k >= 1:
            stage_route(k - 1)
            stage_new(k - 1)
    stage_route(chunks - 1)
    stage_new(chunks - 1)
    for k in range(chunks):
        finish_weights(k)
        finish_owned(k)

    for k in range(chunks):
        some = qr[k].at[pl.ds(0, spots - 1)]
        drain(r[k], sa.at[k])
        drain(cf[k], sc.at[k])
        drain(qd[k], sd.at[k])
        drain(some, sq.at[k])
        drain(some, sf.at[k])
        drain(nn[k], sn.at[k])
    for n in range(3):
        drain(e1, sx.at[n])
    drain(er.at[pl.ds(0, spots - 1)], se)
    drain(er.at[pl.ds(0, spots - 1)], sg)
    drain(er.at[pl.ds(0, spots - 1)], rg)
    drain(e2, le)


def route(tabs, x, a, m, basis, embed, anchor_embed, inner):
    slabs, rows, full = x.shape
    capacity, shards, _, half = a.shape
    spots = shards // PLANES
    lines = spots // inner
    slots = spots * capacity
    ranks = slabs * 3 // 4
    width = half // CHUNKS
    bf16, f32 = jnp.bfloat16, jnp.float32
    vmem = lambda *shape: [pltpu.VMEM(shape, bf16)] * CHUNKS
    sem = pltpu.SemaphoreType.DMA
    whole = (slabs, rows, width)
    most = (ranks, rows, width)
    spread = (spots, capacity, PLANES, rows, width)
    laid = (capacity, lines, PLANES, inner, rows, width)
    factor = (basis.shape[1], embed.shape[1])
    scratch = []
    for shape in (whole,) * 6 + (most, most, spread, laid, laid, spread, most, most, whole, whole):
        scratch += vmem(*shape)
    scratch += [
        pltpu.VMEM(factor, f32),
        pltpu.VMEM((spots, 8, 128), f32),
        pltpu.VMEM((8, 128), f32),
        pltpu.VMEM((4, 8, 128), f32),
        pltpu.VMEM((8, 128), f32),
    ]
    scratch += [sem((CHUNKS,))] * 18
    scratch += [sem(()), sem(()), sem((3,)), sem((3,)), sem(()), sem(()), sem(())]
    vm = pl.BlockSpec(memory_space=pltpu.VMEM)
    hbm = pl.BlockSpec(memory_space=pltpu.HBM)
    keep = lambda array: pltpu.with_memory_space_constraint(array, pltpu.HBM)
    return pl.pallas_call(
        functools.partial(route_kernel, (shards, slabs, slots, ranks, inner, width)),
        out_shape=(
            pltpu.VMEM(a.shape, f32),
            pltpu.VMEM(a.shape, f32),
            pltpu.VMEM(x.shape, bf16),
            pltpu.HBM(factor, f32),
        ),
        in_specs=[pl.BlockSpec(memory_space=pltpu.SMEM), hbm, hbm, hbm, vm, vm, vm],
        out_specs=(vm, vm, vm, hbm),
        scratch_shapes=scratch,
        compiler_params=pltpu.CompilerParams(collective_id=0, has_side_effects=True, vmem_limit_bytes=30 << 20),
    )(tabs, keep(x), keep(a), keep(m), basis, embed, anchor_embed)


def tables(slab_owner, shards, inner, capacity, plane_here, spot_here):
    slabs = slab_owner.shape[0]
    slots = shards // PLANES * capacity
    ranks = slabs * 3 // 4
    ids = jnp.arange(slabs, dtype=jnp.int32)
    plane, spot = place(slab_owner, inner)
    earlier = ids[None, :] < ids[:, None]
    count = lambda mask: jnp.sum((mask & earlier).astype(jnp.int32), axis=1)
    slot = spot * capacity + count(slab_owner[:, None] == slab_owner[None, :])
    rank = count(plane[:, None] == plane[None, :])
    mine = plane == plane_here
    pick = lambda hit, value: jnp.sum(jnp.where(hit, value[None, :], 0), axis=1)
    at_slot = mine[None, :] & (slot[None, :] == jnp.arange(slots, dtype=jnp.int32)[:, None])
    at_rank = rank[None, :] == jnp.arange(ranks, dtype=jnp.int32)[:, None]
    here = spot_here * capacity + jnp.arange(capacity, dtype=jnp.int32)
    used = jnp.any(mine[None, :] & (slot[None, :] == here[:, None]), axis=1)
    tabs = jnp.concatenate(
        [
            pick(at_slot, ids),
            pick(at_slot, rank),
            pick(at_rank & ~mine[None, :], ids),
            pick(at_rank & mine[None, :], slot),
            mine.astype(jnp.int32),
            jnp.where(mine, slot, rank),
            used.astype(jnp.int32),
        ]
    )
    return tabs


def nesterov(anchor_value, moment, mean_value):
    outer_grad = anchor_value - mean_value
    new_moment = MOMENTUM_COEF * moment + outer_grad
    new_anchor = anchor_value - OUTER_RATE * (outer_grad + MOMENTUM_COEF * new_moment)
    return (new_anchor, new_moment)


def on_device(
    replica_weights,
    anchor_slabs,
    momentum_slabs,
    slab_owner,
    replica_embed,
    anchor_embed,
    momentum_embed,
    embed_basis,
):
    rows = replica_weights[0]
    slabs, row_count, width = rows.shape
    half = width // 2
    shards = lax.axis_size("shard")
    inner = INNER[shards]
    capacity = anchor_slabs.shape[1]
    anchor, moment = anchor_slabs[0], momentum_slabs[0]
    plane_here, spot_here = place(lax.axis_index("shard"), inner)
    tabs = tables(slab_owner, shards, inner, capacity, plane_here, spot_here)
    by_rows = lambda slab: slab.reshape(capacity, shards, row_count, half)
    new_anchor, new_moment, new_rows, embed_factor = route(
        tabs, rows, by_rows(anchor), by_rows(moment), embed_basis, replica_embed[0], anchor_embed, inner
    )
    new_anchor, new_moment = new_anchor.reshape(anchor.shape), new_moment.reshape(anchor.shape)
    embed_grad = jnp.dot(embed_basis, embed_factor, precision=lax.Precision.HIGHEST)
    new_anchor_embed, new_momentum_embed = nesterov(
        anchor_embed, momentum_embed, anchor_embed - embed_grad
    )
    new_embed_rows = new_anchor_embed.astype(jnp.bfloat16)
    return (
        new_anchor[None],
        new_moment[None],
        new_rows[None],
        new_anchor_embed,
        new_momentum_embed,
        new_embed_rows[None],
    )


def solution(mesh):
    in_specs = (
        P("group", None, "shard", None),
        P("shard", None, None, "group"),
        P("shard", None, None, "group"),
        P(),
        P("group", "shard", None),
        P("shard", None),
        P("shard", None),
        P("shard", None),
    )
    out_specs = (
        P("shard", None, None, "group"),
        P("shard", None, None, "group"),
        P("group", None, "shard", None),
        P("shard", None),
        P("shard", None),
        P("group", "shard", None),
    )
    return jax.shard_map(
        on_device, mesh=mesh, in_specs=in_specs, out_specs=out_specs, check_vma=False
    )
```

time: 90.5 us -> 75.2 us (0.83)
  other arithmetic: 19.4 us -> 2.69 us
  local copies, waits for them, and re-layouts: 4.51 us -> 7.62 us
  matrix products: 1.91 us -> 0.82 us
    select_n x3 -> x0, other arithmetic: 8.49 us -> none  [the longest x1 5.08 us: on_device(): new_moment = jnp.where(keep, new_moment, moment)]
    convert_element_type x1, other arithmetic: 6.14 us -> 0.01 us  [tables(): used.astype(jnp.int32)]
    unnamed x14 -> x13, local copies, waits for them, and re-layouts: 2.25 us -> 7.53 us
    reshape x2 -> x0, local copies, waits for them, and re-layouts: 1.58 us -> none  [the longest x1 0.93 us: on_device(): embed_factor = factor.reshape(partial_factor.shape)]
    broadcast_in_dim x1 -> x0, other arithmetic: 1.51 us -> none  [on_device(): new_rows[None]]
    dot_general x1 -> x0, matrix products: 1.08 us -> none  [on_device(): jnp.dot(embed_basis.T, anchor_embed / n_group - embed_here / n_group, pre...]
where the time goes in v3:
time: 75.2 us; the launch traced here: 74.8 us
  Pallas kernels  63 us (84%)
  local copies, waits for them, and re-layouts  7.62 us (10%)
  other arithmetic  2.69 us (4%)
  matrix products  0.82 us (1%)
    pallas_call x1, Pallas kernels, route(): pl.pallas_call(functools.partial(route_kernel, (shards, slabs, slots, ran...  63 us
    unnamed x13, local copies, waits for them, and re-layouts  7.53 us

profile of v3, /device:TPU:1, one launch (start us, length us, event | category | flops | bytes accessed | tf_op | source)
XLA Modules:
  0.0 74.8 jit_solution(3157794524367735788)
XLA Ops:
  0.7 0.7 compare_select_fusion
  1.3 0.9 %convert_reduce_fusion = (s32[64]{0:T(128)S(1)}, s32[64]{0:T(128)S(1)}) fusion(s32[64]{0:T(128)S(1)} %compare_select_fusion, s32[64]{0:T(128)} %param.11), kind=kLoop, calls=%fused_computation.6 | loop fusion | flops 36736 | bytes 1024 | tf_op jit(solution)/shard_map/reduce_sum | solution.py:363
  2.2 0.7 fusion.10
  2.9 0.2 and_reduce_fusion
  3.1 0.1 select_reduce_fusion
  3.2 0.1 select_reduce_fusion.2
  3.4 0.1 concatenate.3.tabs
  3.4 0.0 copy-start
  3.4 0.8 %copy-done = f32[12,512]{1,0:T(8,128)S(1)} copy-done((f32[12,512]{1,0:T(8,128)S(1)}, f32[12,512]{1,0:T(8,128)}, u32[]{:S(2)}) %copy-start) | copy-done | bytes 24600
  4.2 0.0 copy-start.1
  4.2 0.7 copy-done.1
  4.9 0.0 copy-start.2
  4.9 0.7 copy-done.2
  5.6 63.0 %shard_map.140 = (f32[2,64,8,1024]{3,2,1,0:T(8,128)S(1)}, f32[2,64,8,1024]{3,2,1,0:T(8,128)S(1)}, bf16[64,8,2048]{2,1,0:T(8,128)(2,1)S(1)}, f32[64,512]{1,0:T(8,128)}) custom-call(s32[354]{0:T(512)S(1)} %concatenate.3.tabs, bf16[64,8,2048]{2,1,0:T(8,128)(2,1)} %bitcast.25, f32[2,64,8,1024]{3,2,1,0:T(8,128)} %bitcast.23, f32[2,64,8,1024]{3,2,1,0:T(8,128)} %bitcast.24, ...), custom_call_target="tpu_custom_call" | custom-call | tf_op jit(solution)/shard_map/pallas_call | solution.py:341
  68.6 2.0 %copy.17 = f32[1,2,512,1024]{3,2,1,0:T(8,128)} copy(f32[1,2,512,1024]{3,2,1,0:T(8,128)S(1)} %bitcast.20) | data formatting | bytes 8388608
  70.6 0.0 copy-start.3
  70.7 0.0 copy-start.4
  70.7 2.0 %copy.18 = f32[1,2,512,1024]{3,2,1,0:T(8,128)} copy(f32[1,2,512,1024]{3,2,1,0:T(8,128)S(1)} %bitcast.19) | data formatting | bytes 8388608
  72.7 0.0 copy-done.3
  72.7 0.0 copy-done.4
  72.7 0.8 %convert_bitcast_fusion = (bf16[1,12,512]{2,1,0:T(8,128)(2,1)}, f32[12,512]{1,0:T(8,128)}, f32[12,512]{1,0:T(8,128)}) fusion(f32[12,512]{1,0:T(8,128)S(1)} %copy-done, f32[12,512]{1,0:T(8,128)S(1)} %copy-done.4, f32[64,512]{1,0:T(8,128)S(1)} %copy-done.3, f32[12,64]{1,0:T(8,128)S(1)} %copy-done.1), kind=kOutput, calls=%fused_computation.19 | convolution fusion | flops 4773888 | bytes 244736 | tf_op jit(solution)/shard_map/dot_general | solution.py:417
  73.5 1.3 %copy.19 = bf16[1,64,8,2048]{3,2,1,0:T(8,128)(2,1)} copy(bf16[1,64,8,2048]{3,2,1,0:T(8,128)(2,1)S(1)} %bitcast.21) | data formatting | bytes 4194304
  (3 shorter events, 0.0 us)
Async XLA Ops:
  3.4 0.8 %copy-start = (f32[12,512]{1,0:T(8,128)S(1)}, f32[12,512]{1,0:T(8,128)}, u32[]{:S(2)}) copy-start(f32[12,512]{1,0:T(8,128)} %anchor_embed.1) | copy-start | bytes 73732
  4.2 0.7 copy-start.1
  4.9 0.7 copy-start.2
  70.6 2.0 %copy-start.3 = (f32[64,512]{1,0:T(8,128)S(1)}, f32[64,512]{1,0:T(8,128)}, u32[]{:S(2)}) copy-start(f32[64,512]{1,0:T(8,128)} %get-tuple-element.13) | copy-start | bytes 393220
  70.7 2.0 %copy-start.4 = (f32[12,512]{1,0:T(8,128)S(1)}, f32[12,512]{1,0:T(8,128)}, u32[]{:S(2)}) copy-start(f32[12,512]{1,0:T(8,128)} %param.14) | copy-start | bytes 73732

commit v4 on v3

--- a/solution.py
+++ b/solution.py
@@ -13,7 +13,8 @@
 MOMENT_COEF = OUTER_RATE * MOMENTUM_COEF * MOMENTUM_COEF
 PLANES = 2
 INNER = {64: 8, 8: 2}
-CHUNKS = 4
+PIECES = (2, 2, 2, 1, 1)
+CHUNKS = len(PIECES)
 UNROLL = 4
 MESH = pl.DeviceIdType.MESH
 
@@ -28,6 +29,11 @@
     return lax.div(spot, inner) * (PLANES * inner) + plane * inner + lax.rem(spot, inner)
 
 
+def cuts(half):
+    unit = half // sum(PIECES)
+    return [unit * sum(PIECES[:k]) for k in range(CHUNKS)], [unit * piece for piece in PIECES]
+
+
 def loop(count, body):
     unroll = UNROLL if count % UNROLL == 0 else 1
 
@@ -47,24 +53,23 @@
     lax.fori_loop(start, stop, step, 0)
 
 
-def route_kernel(sizes, tabs, x, a, m, basis, embed, anchor_embed, na, nm, w_out, e_out, *scratch):
-    shards, slabs, slots, ranks, inner, width = sizes
+def route_kernel(sizes, owners, x, a, m, basis_in, embed_in, anchor_in, na, nm, w_out, e_out, *scratch):
+    shards, slabs, slots, ranks, inner, half = sizes
+    starts, widths = cuts(half)
     chunks = CHUNKS
     spots = shards // PLANES
     capacity = slots // spots
-    half = width * chunks
     bf16, f32 = jnp.bfloat16, jnp.float32
     (xl, xr, xs, xo, r, s, fc, cf, ys, fr, qb, qr, qc, qd, nn, nr) = [
         scratch[i * chunks : (i + 1) * chunks] for i in range(16)
     ]
-    part, er, e1, ex, e2, *sems = scratch[16 * chunks :]
+    part, er, e1, ex, e2, basis, embed, anchor_embed, column, rows_v, tabs, *sems = scratch[16 * chunks :]
     (sa, ra, sc, rc, sq, rq, sd, rd, sf, rf, sn, rn, lx, ly, la, lm, lq, lf) = sems[:18]
-    (se, re, sx, rx, sg, rg, le) = sems[18:]
+    (se, re, sx, rx, sg, rg, le, lt, li) = sems[18:]
 
     group = lax.axis_index("group")
     shard = lax.axis_index("shard")
     plane, spot = place(shard, inner)
-    line, lane = lax.div(spot, inner), lax.rem(spot, inner)
     other = 1 - plane
     partner = (1 - group, shard)
     across = (1 - group, shard_of(spot, other, inner))
@@ -82,20 +87,19 @@
     def drain(ref, sem):
         pltpu.make_async_copy(ref, ref, sem).wait()
 
-    off_fo, off_rk = 0, slots
-    off_fc, off_fp = 2 * slots, 2 * slots + ranks
-    off_in, off_ts = 2 * slots + 2 * ranks, 2 * slots + 2 * ranks + slabs
-    off_used = off_ts + slabs
-
     def cols(k):
-        return pl.ds(k * width, width)
+        return pl.ds(starts[k], widths[k])
 
     def right(k):
-        return pl.ds(half + k * width, width)
-
+        return pl.ds(half + starts[k], widths[k])
+
+    small = ((basis_in, basis), (embed_in, embed), (anchor_in, anchor_embed))
     for k in range(chunks):
         pltpu.make_async_copy(x.at[:, :, cols(k)], xl[k], lx.at[k]).start()
         pltpu.make_async_copy(x.at[:, :, right(k)], xr[k], ly.at[k]).start()
+        if k == 0:
+            for n, (src, dst) in enumerate(small):
+                pltpu.make_async_copy(src, dst, li.at[n]).start()
         pltpu.make_async_copy(a.at[:, :, :, cols(k)], na.at[:, :, :, cols(k)], la.at[k]).start()
         pltpu.make_async_copy(m.at[:, :, :, cols(k)], nm.at[:, :, :, cols(k)], lm.at[k]).start()
 
@@ -110,7 +114,35 @@
     pl.semaphore_wait(barrier, spots - 1 + 3)
 
     def is_left(t):
-        return lax.rem(tabs[off_in + t] + group, 2) == 1
+        return (place(owners[t], inner)[0] == plane) == (group == 0)
+
+    FO, RK, FC, FP, IN, TS, USED = range(7)
+
+    def fill_tables():
+        def put(t):
+            column[pl.ds(t, 1), :] = jnp.full((1, 128), owners[t], jnp.int32)
+
+        loop(slabs, put)
+        owner = column[...]
+        sub = lax.broadcasted_iota(jnp.int32, owner.shape, 0)
+        at = lax.broadcasted_iota(jnp.int32, owner.shape, 1)
+        down = lambda hit, value: jnp.sum(jnp.where(hit, value, 0), axis=0, keepdims=True)
+        count = lambda hit: jnp.sum(jnp.where(hit & (at < sub), 1, 0), axis=1, keepdims=True)
+        own_plane, own_spot = place(owner, inner)
+        row = down(at == sub, owner)
+        row_plane = place(row, inner)[0]
+        slot = own_spot * capacity + count(owner == row)
+        rank = jnp.broadcast_to(count(own_plane == row_plane), owner.shape)
+        mine = own_plane == plane
+        rows_v[pl.ds(FO, 1), :] = jnp.minimum(down(mine & (slot == at), sub), slabs - 1)
+        rows_v[pl.ds(RK, 1), :] = jnp.minimum(down(mine & (slot == at), rank), ranks - 1)
+        rows_v[pl.ds(FC, 1), :] = jnp.minimum(down((own_plane != plane) & (rank == at), sub), slabs - 1)
+        rows_v[pl.ds(FP, 1), :] = jnp.minimum(down(mine & (rank == at), slot), slots - 1)
+        rows_v[pl.ds(IN, 1), :] = down(mine & (at == sub), 1)
+        rows_v[pl.ds(TS, 1), :] = down(at == sub, jnp.where(mine, jnp.minimum(slot, slots - 1), jnp.minimum(rank, ranks - 1)))
+        rows_v[pl.ds(USED, 1), :] = down(mine & (slot == at), 1)
+        pltpu.make_async_copy(rows_v, tabs, lt).start()
+        drain(tabs, lt)
 
     def start_x(k):
         drain(xl[k], lx.at[k])
@@ -133,24 +165,26 @@
             z, b, i = lax.div(n, PLANES * inner), lax.rem(lax.div(n, inner), PLANES), lax.rem(n, inner)
             for c in range(capacity):
                 value = (1.0 - GRAD_COEF) * na[c, n, :, cols(k)] - MOMENT_COEF * nm[c, n, :, cols(k)]
-                qb[k][c, z, b, i] = value.astype(bf16)
+                qb[k][z * inner + i, c, b] = value.astype(bf16)
 
         loop(shards, base)
 
         def send_q(i):
             d, device = peer(i)
             remote(
-                qb[k].at[:, lax.div(d, inner), :, lax.rem(d, inner)], qr[k].at[spot], sq.at[k], rq.at[k], device
+                qb[k].at[d], qr[k].at[spot], sq.at[k], rq.at[k], device
             ).start()
 
         each(1, spots, send_q)
-        pltpu.make_async_copy(qb[k].at[:, line, :, lane], qr[k].at[spot], lq.at[k]).start()
+        pltpu.make_async_copy(qb[k].at[spot], qr[k].at[spot], lq.at[k]).start()
 
     def tile(ref, d):
         per = ref.shape[1] // 128
         return ref.at[pl.ds(lax.div(d, per) * 8, 8), pl.ds(pl.multiple_of(lax.rem(d, per) * 128, 128), 128)]
 
     def factor_start():
+        for n, (_, dst) in enumerate(small):
+            drain(dst, li.at[n])
         diff = 0.5 * anchor_embed[...] - 0.5 * embed[...].astype(f32)
         part[...] = lax.dot_general(
             basis[...], diff, (((0,), (0,)), ((), ())), precision=lax.Precision.HIGHEST, preferred_element_type=f32
@@ -173,13 +207,13 @@
         loop(slabs, add)
 
         def pick_cross(i):
-            fc[k][i] = s[k][tabs[off_fc + i]]
+            fc[k][i] = s[k][tabs[FC, i]]
 
         loop(ranks, pick_cross)
         remote(fc[k], cf[k], sc.at[k], rc.at[k], across).start()
 
         def pick_own(j):
-            ys[k][lax.div(j, capacity), lax.rem(j, capacity), plane] = s[k][tabs[off_fo + j]]
+            ys[k][lax.div(j, capacity), lax.rem(j, capacity), plane] = s[k][tabs[FO, j]]
 
         loop(slots, pick_own)
 
@@ -188,7 +222,7 @@
         drain(qr[k].at[0], lq.at[k])
 
         def pick(i):
-            j = tabs[off_fp + i]
+            j = tabs[FP, i]
             qc[k][i] = qr[k][lax.div(j, capacity), lax.rem(j, capacity), other]
 
         loop(ranks, pick)
@@ -198,23 +232,23 @@
         drain(cf[k], rc.at[k])
 
         def pick(j):
-            ys[k][lax.div(j, capacity), lax.rem(j, capacity), other] = cf[k][tabs[off_rk + j]]
+            ys[k][lax.div(j, capacity), lax.rem(j, capacity), other] = cf[k][tabs[RK, j]]
 
         loop(slots, pick)
 
         def send(i):
             d, device = peer(i)
-            remote(ys[k].at[d], fr[k].at[:, line, :, lane], sf.at[k], rf.at[k], device).start()
+            remote(ys[k].at[d], fr[k].at[spot], sf.at[k], rf.at[k], device).start()
 
         each(1, spots, send)
-        pltpu.make_async_copy(ys[k].at[spot], fr[k].at[:, line, :, lane], lf.at[k]).start()
+        pltpu.make_async_copy(ys[k].at[spot], fr[k].at[spot], lf.at[k]).start()
 
     def stage_new(k):
         drain(qd[k], rd.at[k])
 
         def combine(t):
-            own = tabs[off_in + t]
-            where = tabs[off_ts + t]
+            own = tabs[IN, t]
+            where = tabs[TS, t]
             j = where * own
             here = qr[k][lax.div(j, capacity), lax.rem(j, capacity), plane]
             there = qd[k][where * (1 - own)]
@@ -232,9 +266,9 @@
         def step(n):
             z, b, i = lax.div(n, PLANES * inner), lax.rem(lax.div(n, inner), PLANES), lax.rem(n, inner)
             for c in range(capacity):
-                used = tabs[off_used + c] == 1
+                used = tabs[USED, spot * capacity + c] == 1
                 anchor, moment = na[c, n, :, cols(k)], nm[c, n, :, cols(k)]
-                new_anchor, new_moment = nesterov(anchor, moment, 0.5 * fr[k][c, z, b, i].astype(f32))
+                new_anchor, new_moment = nesterov(anchor, moment, 0.5 * fr[k][z * inner + i, c, b].astype(f32))
                 na[c, n, :, cols(k)] = jnp.where(used, new_anchor, anchor)
                 nm[c, n, :, cols(k)] = jnp.where(used, new_moment, moment)
 
@@ -275,6 +309,7 @@
         start_q(k)
         if k == 0:
             factor_start()
+    fill_tables()
     for k in range(chunks):
         stage_sum(k)
         stage_q(k)
@@ -307,80 +342,52 @@
     drain(e2, le)
 
 
-def route(tabs, x, a, m, basis, embed, anchor_embed, inner):
+def route(owners, x, a, m, basis, embed, anchor_embed, inner):
     slabs, rows, full = x.shape
     capacity, shards, _, half = a.shape
     spots = shards // PLANES
-    lines = spots // inner
     slots = spots * capacity
     ranks = slabs * 3 // 4
-    width = half // CHUNKS
     bf16, f32 = jnp.bfloat16, jnp.float32
-    vmem = lambda *shape: [pltpu.VMEM(shape, bf16)] * CHUNKS
     sem = pltpu.SemaphoreType.DMA
-    whole = (slabs, rows, width)
-    most = (ranks, rows, width)
-    spread = (spots, capacity, PLANES, rows, width)
-    laid = (capacity, lines, PLANES, inner, rows, width)
+    whole = (slabs, rows)
+    most = (ranks, rows)
+    spread = (spots, capacity, PLANES, rows)
     factor = (basis.shape[1], embed.shape[1])
     scratch = []
-    for shape in (whole,) * 6 + (most, most, spread, laid, laid, spread, most, most, whole, whole):
-        scratch += vmem(*shape)
+    for shape in (whole,) * 6 + (most, most, spread, spread, spread, spread, most, most, whole, whole):
+        scratch += [pltpu.VMEM((*shape, width), bf16) for width in cuts(half)[1]]
     scratch += [
         pltpu.VMEM(factor, f32),
         pltpu.VMEM((spots, 8, 128), f32),
         pltpu.VMEM((8, 128), f32),
         pltpu.VMEM((4, 8, 128), f32),
         pltpu.VMEM((8, 128), f32),
+        pltpu.VMEM(basis.shape, f32),
+        pltpu.VMEM(embed.shape, bf16),
+        pltpu.VMEM(anchor_embed.shape, f32),
+        pltpu.VMEM((slabs, 128), jnp.int32),
+        pltpu.VMEM((8, 128), jnp.int32),
+        pltpu.SMEM((8, 128), jnp.int32),
     ]
     scratch += [sem((CHUNKS,))] * 18
-    scratch += [sem(()), sem(()), sem((3,)), sem((3,)), sem(()), sem(()), sem(())]
+    scratch += [sem(()), sem(()), sem((3,)), sem((3,)), sem(()), sem(()), sem(()), sem(()), sem((3,))]
     vm = pl.BlockSpec(memory_space=pltpu.VMEM)
     hbm = pl.BlockSpec(memory_space=pltpu.HBM)
     keep = lambda array: pltpu.with_memory_space_constraint(array, pltpu.HBM)
     return pl.pallas_call(
-        functools.partial(route_kernel, (shards, slabs, slots, ranks, inner, width)),
+        functools.partial(route_kernel, (shards, slabs, slots, ranks, inner, half)),
         out_shape=(
             pltpu.VMEM(a.shape, f32),
             pltpu.VMEM(a.shape, f32),
             pltpu.VMEM(x.shape, bf16),
             pltpu.HBM(factor, f32),
         ),
-        in_specs=[pl.BlockSpec(memory_space=pltpu.SMEM), hbm, hbm, hbm, vm, vm, vm],
+        in_specs=[pl.BlockSpec(memory_space=pltpu.SMEM)] + [hbm] * 6,
         out_specs=(vm, vm, vm, hbm),
         scratch_shapes=scratch,
         compiler_params=pltpu.CompilerParams(collective_id=0, has_side_effects=True, vmem_limit_bytes=30 << 20),
-    )(tabs, keep(x), keep(a), keep(m), basis, embed, anchor_embed)
-
-
-def tables(slab_owner, shards, inner, capacity, plane_here, spot_here):
-    slabs = slab_owner.shape[0]
-    slots = shards // PLANES * capacity
-    ranks = slabs * 3 // 4
-    ids = jnp.arange(slabs, dtype=jnp.int32)
-    plane, spot = place(slab_owner, inner)
-    earlier = ids[None, :] < ids[:, None]
-    count = lambda mask: jnp.sum((mask & earlier).astype(jnp.int32), axis=1)
-    slot = spot * capacity + count(slab_owner[:, None] == slab_owner[None, :])
-    rank = count(plane[:, None] == plane[None, :])
-    mine = plane == plane_here
-    pick = lambda hit, value: jnp.sum(jnp.where(hit, value[None, :], 0), axis=1)
-    at_slot = mine[None, :] & (slot[None, :] == jnp.arange(slots, dtype=jnp.int32)[:, None])
-    at_rank = rank[None, :] == jnp.arange(ranks, dtype=jnp.int32)[:, None]
-    here = spot_here * capacity + jnp.arange(capacity, dtype=jnp.int32)
-    used = jnp.any(mine[None, :] & (slot[None, :] == here[:, None]), axis=1)
-    tabs = jnp.concatenate(
-        [
-            pick(at_slot, ids),
-            pick(at_slot, rank),
-            pick(at_rank & ~mine[None, :], ids),
-            pick(at_rank & mine[None, :], slot),
-            mine.astype(jnp.int32),
-            jnp.where(mine, slot, rank),
-            used.astype(jnp.int32),
-        ]
-    )
-    return tabs
+    )(owners, *map(keep, (x, a, m, basis, embed, anchor_embed)))
 
 
 def nesterov(anchor_value, moment, mean_value):
@@ -407,11 +414,9 @@
     inner = INNER[shards]
     capacity = anchor_slabs.shape[1]
     anchor, moment = anchor_slabs[0], momentum_slabs[0]
-    plane_here, spot_here = place(lax.axis_index("shard"), inner)
-    tabs = tables(slab_owner, shards, inner, capacity, plane_here, spot_here)
     by_rows = lambda slab: slab.reshape(capacity, shards, row_count, half)
     new_anchor, new_moment, new_rows, embed_factor = route(
-        tabs, rows, by_rows(anchor), by_rows(moment), embed_basis, replica_embed[0], anchor_embed, inner
+        slab_owner, rows, by_rows(anchor), by_rows(moment), embed_basis, replica_embed[0], anchor_embed, inner
     )
     new_anchor, new_moment = new_anchor.reshape(anchor.shape), new_moment.reshape(anchor.shape)
     embed_grad = jnp.dot(embed_basis, embed_factor, precision=lax.Precision.HIGHEST)

time: 75.2 us -> 72 us (0.957)
  other arithmetic: 2.69 us -> 0 us
  local copies, waits for them, and re-layouts: 7.62 us -> 6 us
  matrix products: 0.82 us -> 1.73 us
    unnamed x13 -> x11, local copies, waits for them, and re-layouts: 7.53 us -> 6 us
    reduce_sum x3 -> x0, other arithmetic: 1.14 us -> none  [the longest x1 0.91 us: tables(): count = lambda mask: jnp.sum((mask & earlier).astype(jnp.int32), axis=1)]
    dot_general x1, matrix products: 0.82 us -> 1.73 us  [on_device(): jnp.dot(embed_basis, embed_factor, precision=lax.Precision.HIGHEST)]
where the time goes in v4:
time: 72 us; the launch traced here: 71.9 us
  Pallas kernels  63.5 us (88%)
  local copies, waits for them, and re-layouts  6 us (8%)
  matrix products  1.73 us (2%)
    pallas_call x1, Pallas kernels, route(): pl.pallas_call(functools.partial(route_kernel, (shards, slabs, slots, ran...  63.5 us
    unnamed x11, local copies, waits for them, and re-layouts  6 us
    dot_general x1, matrix products, on_device(): jnp.dot(embed_basis, embed_factor, precision=lax.Precision.HIGHEST)  1.73 us

profile of v4, /device:TPU:1, one launch (start us, length us, event | category | flops | bytes accessed | tf_op | source)
XLA Modules:
  0.0 71.9 jit_solution(13287024869465130958)
XLA Ops:
  0.6 0.0 copy-start
  0.6 0.6 copy-done
  1.3 0.0 copy-start.1
  1.3 0.0 copy-start.2
  1.3 0.0 copy-start.3
  1.3 63.5 %shard_map.127 = (f32[2,64,8,1024]{3,2,1,0:T(8,128)S(1)}, f32[2,64,8,1024]{3,2,1,0:T(8,128)S(1)}, bf16[64,8,2048]{2,1,0:T(8,128)(2,1)S(1)}, f32[64,512]{1,0:T(8,128)}) custom-call(s32[64]{0:T(128)S(1)} %copy-done, bf16[64,8,2048]{2,1,0:T(8,128)(2,1)} %bitcast.24, f32[2,64,8,1024]{3,2,1,0:T(8,128)} %bitcast.22, f32[2,64,8,1024]{3,2,1,0:T(8,128)} %bitcast.23, ...), custom_call_target="tpu_custom_call" | custom-call | tf_op jit(solution)/shard_map/pallas_call | solution.py:378
  64.8 0.0 copy-done.1
  64.8 0.0 copy-done.2
  64.8 0.0 copy-done.3
  64.8 1.7 %convert_bitcast_fusion = (bf16[1,12,512]{2,1,0:T(8,128)(2,1)}, f32[12,512]{1,0:T(8,128)}, f32[12,512]{1,0:T(8,128)}) fusion(f32[12,512]{1,0:T(8,128)S(1)} %copy-done.1, f32[12,512]{1,0:T(8,128)S(1)} %copy-done.3, f32[64,512]{1,0:T(8,128)} %get-tuple-element.13, f32[12,64]{1,0:T(8,128)S(1)} %copy-done.2), kind=kOutput, calls=%fused_computation.5 | convolution fusion | flops 4773888 | bytes 244736 | tf_op jit(solution)/shard_map/dot_general | solution.py:422
  66.5 2.0 %copy.17 = f32[1,2,512,1024]{3,2,1,0:T(8,128)} copy(f32[1,2,512,1024]{3,2,1,0:T(8,128)S(1)} %bitcast.20) | data formatting | bytes 8388608
  68.6 2.0 %copy.18 = f32[1,2,512,1024]{3,2,1,0:T(8,128)} copy(f32[1,2,512,1024]{3,2,1,0:T(8,128)S(1)} %bitcast.19) | data formatting | bytes 8388608
  70.6 1.3 %copy.19 = bf16[1,64,8,2048]{3,2,1,0:T(8,128)(2,1)} copy(bf16[1,64,8,2048]{3,2,1,0:T(8,128)(2,1)S(1)} %bitcast.21) | data formatting | bytes 4194304
Async XLA Ops:
  0.6 0.7 copy-start
  1.3 63.5 %copy-start.1 = (f32[12,512]{1,0:T(8,128)S(1)}, f32[12,512]{1,0:T(8,128)}, u32[]{:S(2)}) copy-start(f32[12,512]{1,0:T(8,128)} %anchor_in.1) | copy-start | bytes 73732
  1.3 63.5 %copy-start.2 = (f32[12,64]{1,0:T(8,128)S(1)}, f32[12,64]{1,0:T(8,128)}, u32[]{:S(2)}) copy-start(f32[12,64]{1,0:T(8,128)} %basis_in.1) | copy-start | bytes 9220
  1.3 63.5 %copy-start.3 = (f32[12,512]{1,0:T(8,128)S(1)}, f32[12,512]{1,0:T(8,128)}, u32[]{:S(2)}) copy-start(f32[12,512]{1,0:T(8,128)} %param.14) | copy-start | bytes 73732
